TPU v7x, 32 devices: a whole 2x2x4 slice. The times are simulated.
32 devices in a mesh: wide: 8 (over z, y), narrow: 4 (over x, core).
Axes of the slice: x: 2, y: 2, z: 4, core: 2. Of those that a mesh axis runs over, the one named last changes fastest.
Arguments:
- tokens: bfloat16 [64, 512, 768], P(('wide', 'narrow')), may hold values from -6 to 6
- segment_ids: int32 [64, 512], P(('wide', 'narrow')), may hold values from 0 to 3, never falling along the last dimension, each value on 1 to 256 neighbouring positions
- cotangent: bfloat16 [64, 512, 768], P(('wide', 'narrow')), may hold values from -6 to 6
- blocks: float32 [12, 768, 768], P(None, ('wide', 'narrow'))
- vectors: float32 [13, 768], P(None, ('wide', 'narrow'))
- stat_left: float32 [32, 768, 768], P(('wide', 'narrow'))
- stat_right: float32 [32, 768, 768], P(('wide', 'narrow'))
- root_left: float32 [32, 768, 768], P(('wide', 'narrow'))
- root_right: float32 [32, 768, 768], P(('wide', 'narrow'))
- vec_stat: float32 [13, 768], P(None, ('wide', 'narrow')), may hold values from 0.5 to 4
- owners: int32 [12], replicated, may hold values from 0 to 31, as said below
Outputs:
- output: bfloat16 [64, 512, 768], P(('wide', 'narrow'))
- grad_tokens: bfloat16 [64, 512, 768], P(('wide', 'narrow'))
- clipped_blocks: float32 [12, 768, 768], P(None, ('wide', 'narrow'))
- clipped_vectors: float32 [13, 768], P(None, ('wide', 'narrow'))
- grad_norm: float32 [], replicated
- new_left: float32 [32, 768, 768], P(('wide', 'narrow'))
- new_right: float32 [32, 768, 768], P(('wide', 'narrow'))
- new_vec_stat: float32 [13, 768], P(None, ('wide', 'narrow'))
- new_blocks: float32 [12, 768, 768], P(None, ('wide', 'narrow'))
- new_vectors: float32 [13, 768], P(None, ('wide', 'narrow'))
- blocks_copy: bfloat16 [12, 768, 768], P(None, ('wide', 'narrow'))
- vectors_copy: bfloat16 [13, 768], P(None, ('wide', 'narrow'))
Inputs may be any that keep to these rules, and one draw needn't show every extreme that they name: `owners`: distinct device numbers; device 0 and device 32 - 1 are always among them. `segment_ids`: within each row never falling, each segment at most 256 tokens.
All inputs are finite; a program needn't handle non-finite values.
Results may differ from a plain program's by a relative error of at most 0.007.
The roundings to bfloat16 on the way count: a program that leaves them out, or rounds other values in their place, can miss the bound.
Values may be sent and summed in bfloat16 or wider, within the bound.
No kernel may reach another device: no remote copies, remote signals or barrier semaphores. Data moves between devices by JAX's collectives and lax.ppermute only.
A program may use at most 256 MiB of HBM per device.

v0:
```python
import math

import jax
import jax.numpy as jnp
from jax import lax
from jax.sharding import PartitionSpec as P

H = 12
FF = 3072
ROT = 16
NPARAM = 7087872


highest = lax.Precision.HIGHEST
clip_level = 1.0
matrix_rate = 0.03
vector_rate = 0.2
decay_beta = 0.5
norm_epsilon = 1e-05


def layer_norm(values, gain, shift):
    centre = jnp.mean(values, axis=-1, keepdims=True)
    centred = values - centre
    spread = jnp.mean(centred * centred, axis=-1, keepdims=True)
    return centred * lax.rsqrt(spread + norm_epsilon) * gain + shift


def rotary_tables(segment_ids):
    length = segment_ids.shape[-1]
    places = jnp.broadcast_to(jnp.arange(length, dtype=jnp.int32), segment_ids.shape)
    earlier = jnp.concatenate([segment_ids[..., :1] - 1, segment_ids[..., :-1]], axis=-1)
    starts = lax.cummax(jnp.where(segment_ids != earlier, places, 0), axis=segment_ids.ndim - 1)
    offset = (places - starts).astype(jnp.float32)
    half_rot = ROT // 2
    rates = jnp.power(10000.0, -2.0 * jnp.arange(half_rot, dtype=jnp.float32) / ROT)
    angles = offset[..., None] * rates
    angles = jnp.concatenate([angles, angles], axis=-1)
    return (jnp.cos(angles), jnp.sin(angles))


def rotate(values, cosine, sine):
    rotary_part = values[..., :ROT]
    first_half = rotary_part[..., : ROT // 2]
    second_half = rotary_part[..., ROT // 2 :]
    turned = jnp.concatenate([-second_half, first_half], axis=-1)
    return jnp.concatenate([rotary_part * cosine + turned * sine, values[..., ROT:]], axis=-1)


def causal_mask(segment_row):
    places = jnp.arange(segment_row.shape[0])
    return (segment_row[:, None] == segment_row[None, :]) & (places[:, None] >= places[None, :])


def gelu_exact(values):
    return jax.nn.gelu(values, approximate=False)


def masked_scores(query_row, key_row, segment_row):
    scores = (
        jnp.einsum("qhd,khd->hqk", query_row, key_row, preferred_element_type=jnp.float32) * 0.125
    )
    return jnp.where(causal_mask(segment_row)[None], scores, -1e30)


def attend_forward(row_parts):
    query_row, key_row, value_row, segment_row = row_parts
    scores = masked_scores(query_row, key_row, segment_row)
    top_score = jnp.max(scores, axis=-1, keepdims=True)
    expected = jnp.exp(scores - top_score)
    row_total = jnp.sum(expected, axis=-1, keepdims=True)
    soft_weights = expected / row_total
    mixed = jnp.einsum(
        "hqk,khd->qhd",
        soft_weights.astype(jnp.bfloat16),
        value_row,
        preferred_element_type=jnp.float32,
    )
    return (mixed, (top_score + jnp.log(row_total))[..., 0])


def attend_backward(row_parts):
    query_row, key_row, value_row, grad_row, log_total, segment_row = row_parts
    scores = masked_scores(query_row, key_row, segment_row)
    soft_weights = jnp.exp(scores - log_total[..., None])
    grad_soft = jnp.einsum("qhd,khd->hqk", grad_row, value_row, preferred_element_type=jnp.float32)
    inner_sum = jnp.sum(soft_weights * grad_soft, axis=-1, keepdims=True)
    grad_scores = (soft_weights * (grad_soft - inner_sum)).astype(jnp.bfloat16)
    grad_query = (
        jnp.einsum("hqk,khd->qhd", grad_scores, key_row, preferred_element_type=jnp.float32) * 0.125
    )
    grad_key = (
        jnp.einsum("hqk,qhd->khd", grad_scores, query_row, preferred_element_type=jnp.float32)
        * 0.125
    )
    grad_value = jnp.einsum(
        "hqk,qhd->khd",
        soft_weights.astype(jnp.bfloat16),
        grad_row,
        preferred_element_type=jnp.float32,
    )
    return (grad_query, grad_key, grad_value)


def per_device(
    tokens,
    segment_ids,
    cotangent,
    blocks,
    vectors,
    stat_left,
    stat_right,
    root_left,
    root_right,
    vec_stat,
    owners,
):
    rows_here, seq_len, model_width = tokens.shape
    token_count = rows_here * seq_len
    head_size = model_width // H
    splits = FF // model_width
    weights, vecs_low = (
        lax.all_gather(blocks.astype(jnp.bfloat16), ("wide", "narrow"), axis=1, tiled=True),
        lax.all_gather(vectors.astype(jnp.bfloat16), ("wide", "narrow"), axis=1, tiled=True),
    )
    vecs = vecs_low.astype(jnp.float32)
    flat_tokens = tokens.reshape(token_count, model_width).astype(jnp.float32)
    normed_one, norm_one_back = jax.vjp(layer_norm, flat_tokens, vecs[0], vecs[1])
    input_one = normed_one.astype(jnp.bfloat16)
    projected = (
        jnp.einsum("nd,kde->nke", input_one, weights[0:3], preferred_element_type=jnp.float32)
        + vecs[4:7][None]
    )
    split_heads = projected.reshape(rows_here, seq_len, 3, H, head_size)
    cosine, sine = rotary_tables(segment_ids)

    def turn(values):
        return rotate(values, cosine[:, :, None, :], sine[:, :, None, :])

    query_rot, turn_back = jax.vjp(turn, split_heads[:, :, 0])
    queries = query_rot.astype(jnp.bfloat16)
    keys_rot = turn(split_heads[:, :, 1]).astype(jnp.bfloat16)
    values_low = split_heads[:, :, 2].astype(jnp.bfloat16)
    mixed, log_total = lax.map(attend_forward, (queries, keys_rot, values_low, segment_ids))
    mixed_low = mixed.reshape(token_count, model_width).astype(jnp.bfloat16)
    attended = jnp.dot(mixed_low, weights[3], preferred_element_type=jnp.float32) + vecs[7]
    normed_two, norm_two_back = jax.vjp(layer_norm, flat_tokens, vecs[2], vecs[3])
    input_two = normed_two.astype(jnp.bfloat16)
    hidden_pre = (
        jnp.einsum(
            "nd,kdf->nkf", input_two, weights[4 : 4 + splits], preferred_element_type=jnp.float32
        )
        + vecs[8 : 8 + splits][None]
    )
    activated, gelu_back = jax.vjp(gelu_exact, hidden_pre)
    active_low = activated.astype(jnp.bfloat16)
    feed = (
        jnp.einsum(
            "nkf,kfd->nd",
            active_low,
            weights[4 + splits : 4 + 2 * splits],
            preferred_element_type=jnp.float32,
        )
        + vecs[8 + splits]
    )
    output = (
        (flat_tokens + attended + feed)
        .astype(jnp.bfloat16)
        .reshape(rows_here, seq_len, model_width)
    )
    back_weights = lax.all_gather(
        blocks.astype(jnp.bfloat16), ("wide", "narrow"), axis=1, tiled=True
    )
    grad_out = cotangent.reshape(token_count, model_width)
    grad_wide = grad_out.astype(jnp.float32)
    bias_total = jnp.sum(grad_wide, axis=0)
    grad_down = jnp.einsum("nkf,nd->kfd", active_low, grad_out, preferred_element_type=jnp.float32)
    grad_active = jnp.einsum(
        "nd,kfd->nkf",
        grad_out,
        back_weights[4 + splits : 4 + 2 * splits],
        preferred_element_type=jnp.float32,
    )
    (grad_hidden,) = gelu_back(grad_active)
    grad_hidden_low = grad_hidden.astype(jnp.bfloat16)
    grad_up_bias = jnp.sum(grad_hidden_low.astype(jnp.float32), axis=0)
    grad_up = jnp.einsum(
        "nd,nkf->kdf", input_two, grad_hidden_low, preferred_element_type=jnp.float32
    )
    grad_normed_two = jnp.einsum(
        "nkf,kdf->nd",
        grad_hidden_low,
        back_weights[4 : 4 + splits],
        preferred_element_type=jnp.float32,
    )
    grad_from_two, grad_gain_two, grad_shift_two = norm_two_back(grad_normed_two)
    grad_outproj = jnp.einsum("ne,nd->ed", mixed_low, grad_out, preferred_element_type=jnp.float32)
    grad_mixed = jnp.einsum(
        "nd,ed->ne", grad_out, back_weights[3], preferred_element_type=jnp.float32
    )
    grad_mixed = grad_mixed.astype(jnp.bfloat16).reshape(rows_here, seq_len, H, head_size)
    grad_query, grad_key, grad_value = lax.map(
        attend_backward, (queries, keys_rot, values_low, grad_mixed, log_total, segment_ids)
    )
    (grad_query_pre,) = turn_back(grad_query)
    (grad_key_pre,) = turn_back(grad_key)
    grad_projected = jnp.stack([grad_query_pre, grad_key_pre, grad_value], axis=2)
    grad_projected = grad_projected.reshape(token_count, 3, model_width).astype(jnp.bfloat16)
    grad_qkv_bias = jnp.sum(grad_projected.astype(jnp.float32), axis=0)
    grad_qkv = jnp.einsum(
        "nd,nke->kde", input_one, grad_projected, preferred_element_type=jnp.float32
    )
    grad_normed_one = jnp.einsum(
        "nke,kde->nd", grad_projected, back_weights[0:3], preferred_element_type=jnp.float32
    )
    grad_from_one, grad_gain_one, grad_shift_one = norm_one_back(grad_normed_one)
    grad_input = (
        (grad_wide + grad_from_one + grad_from_two)
        .astype(jnp.bfloat16)
        .reshape(rows_here, seq_len, model_width)
    )
    grad_blocks = jnp.concatenate([grad_qkv, grad_outproj[None], grad_up, grad_down], axis=0)
    grad_vectors = jnp.concatenate(
        [
            jnp.stack([grad_gain_one, grad_shift_one, grad_gain_two, grad_shift_two]),
            grad_qkv_bias,
            bias_total[None],
            grad_up_bias,
            bias_total[None],
        ],
        axis=0,
    )
    shard_blocks, shard_vectors = (
        lax.psum_scatter(grad_blocks, ("wide", "narrow"), scatter_dimension=1, tiled=True),
        lax.psum_scatter(grad_vectors, ("wide", "narrow"), scatter_dimension=1, tiled=True),
    )
    local_squares = jnp.sum(shard_blocks * shard_blocks) + jnp.sum(shard_vectors * shard_vectors)
    squares = lax.psum(local_squares, ("wide", "narrow"))
    grad_norm = jnp.sqrt(squares)
    factor = jnp.minimum(1.0, clip_level / grad_norm)
    root_count = math.sqrt(NPARAM)
    slot_count = lax.axis_size(("wide", "narrow"))
    my_index = lax.axis_index(("wide", "narrow"))
    ownership = (owners[None, :] == jnp.arange(slot_count, dtype=jnp.int32)[:, None]).astype(
        jnp.float32
    )
    has_block = jnp.any(owners == my_index)
    clipped_blocks = shard_blocks * factor
    scaled_rows = clipped_blocks * root_count
    outgoing = jnp.einsum("jb,brd->jrd", ownership, scaled_rows, precision=highest)
    arrived = lax.all_to_all(
        outgoing.astype(jnp.bfloat16), ("wide", "narrow"), split_axis=0, concat_axis=0, tiled=True
    ).astype(outgoing.dtype)
    owned_block = arrived.reshape(model_width, model_width)
    left_old = stat_left[0]
    right_old = stat_right[0]
    left_next = decay_beta * left_old + (1.0 - decay_beta) * (
        jnp.dot(owned_block, owned_block.T, precision=highest) / model_width
    )
    right_next = decay_beta * right_old + (1.0 - decay_beta) * (
        jnp.dot(owned_block.T, owned_block, precision=highest) / model_width
    )
    precond = jnp.dot(
        jnp.dot(root_left[0], owned_block, precision=highest), root_right[0], precision=highest
    )
    new_left = jnp.where(has_block, left_next, left_old)[None]
    new_right = jnp.where(has_block, right_next, right_old)[None]
    returned = lax.all_to_all(
        precond.reshape(slot_count, model_width // slot_count, model_width).astype(jnp.bfloat16),
        ("wide", "narrow"),
        split_axis=0,
        concat_axis=0,
        tiled=True,
    ).astype(jnp.float32)
    update_rows = jnp.einsum("jb,jrd->brd", ownership, returned, precision=highest)
    new_blocks = blocks - matrix_rate * update_rows
    clipped_vectors = shard_vectors * factor
    scaled_vectors = clipped_vectors * root_count
    new_vec_stat = decay_beta * vec_stat + (1.0 - decay_beta) * (scaled_vectors * scaled_vectors)
    new_vectors = vectors - vector_rate * scaled_vectors * lax.rsqrt(new_vec_stat)
    return (
        output,
        grad_input,
        clipped_blocks,
        clipped_vectors,
        grad_norm,
        new_left,
        new_right,
        new_vec_stat,
        new_blocks,
        new_vectors,
        new_blocks.astype(jnp.bfloat16),
        new_vectors.astype(jnp.bfloat16),
    )


def solution(mesh):
    placed = (
        P(("wide", "narrow"), None, None),
        P(("wide", "narrow"), None),
        P(("wide", "narrow"), None, None),
        P(None, ("wide", "narrow"), None),
        P(None, ("wide", "narrow")),
        P(("wide", "narrow"), None, None),
        P(("wide", "narrow"), None, None),
        P(("wide", "narrow"), None, None),
        P(("wide", "narrow"), None, None),
        P(None, ("wide", "narrow")),
        P(),
    )
    return jax.shard_map(
        per_device,
        mesh=mesh,
        in_specs=placed,
        out_specs=(
            P(("wide", "narrow"), None, None),
            P(("wide", "narrow"), None, None),
            P(None, ("wide", "narrow"), None),
            P(None, ("wide", "narrow")),
            P(),
            P(("wide", "narrow"), None, None),
            P(("wide", "narrow"), None, None),
            P(None, ("wide", "narrow")),
            P(None, ("wide", "narrow"), None),
            P(None, ("wide", "narrow")),
            P(None, ("wide", "narrow"), None),
            P(None, ("wide", "narrow")),
        ),
        check_vma=False,
    )
```

profile of v0, /device:TPU:0, one launch (start us, length us, event | category | flops | bytes accessed | tf_op | source)
XLA Modules:
  0.0 1062.9 jit_solution(6918758422093212112)
XLA Ops:
  10.2 44.0 %all-gather = bf16[32,24,13]{1,2,0:T(8,128)(2,1)S(1)} all-gather(bf16[1,24,13]{1,2,0:T(8,128)(2,1)S(1)} %convert_bitcast_fusion), channel_id=1, replica_groups=mesh['wide'=8,'narrow'=4] {'wide','narrow'}, dimensions={0}, use_global_device_ids=true | all-gather | bytes 20592 | tf_op jit(solution)/shard_map/all_gather | solution.py:124
  67.8 49.8 %all-gather.3.cloned.1.call-done = bf16[12,768,768]{2,1,0:T(8,128)(2,1)} async-done(((bf16[12,24,768]{2,1,0:T(8,128)(2,1)}), bf16[12,768,768]{2,1,0:T(8,128)(2,1)}) %all-gather.3.cloned.1.call-update) | async-done | bytes 14155792 | tf_op jit(solution)/shard_map/all_gather | solution.py:123
  117.6 10.0 broadcast_add_fusion
  127.6 9.6 copy.123
  137.2 13.5 %reshape.302 = f32[2,512,3,12,64]{1,0,4,3,2:T(2,128)} reshape(f32[1024,3,768]{0,2,1:T(8,128)} %copy.123) | data formatting | bytes 18874368 | tf_op jit(solution)/shard_map/reshape | solution.py:134
  191.2 23.5 %while.26 = (s32[]{:T(128)}, bf16[2,512,12,64]{1,3,2,0:T(8,128)(2,1)}, f32[2,12,512]{2,1,0:T(8,128)S(1)}, bf16[2,512,12,64]{1,3,2,0:T(8,128)(2,1)}, s32[2,512]{1...) while((s32[]{:T(128)}, ...), condition=%wide.region_7.8_spmd, body=%wide.region_4.7_spmd.sunk | while | flops 843835392 | bytes 42958948 | solution.py:144
  216.0 176.0 %while.27 = (s32[]{:T(128)}, f32[2,512,12,64]{1,0,3,2:T(2,128)}, f32[2,512,12,64]{1,0,3,2:T(2,128)}, bf16[2,512,12,64]{1,3,2,0:T(8,128)(2,1)}, bf16[2,512,12,64]...) while((s32[]{:T(128)}, f32[2,512,12,64]{1,0,3,2:T(2,128)}, ...), condition=%wide.region_10.11_spmd, body=%wide.region_8.10_spmd.sunk | while | flops 2062018560 | bytes 143590656 | solution.py:202
  223.7 6.9 multiply_reduce_fusion.4
  230.5 7.1 multiply_convert_fusion.3
  246.4 28.8 %dynamic_update_slice.29 = f32[2,512,12,64]{1,0,3,2:T(2,128)} dynamic-update-slice(f32[2,512,12,64]{1,0,3,2:T(2,128)} %get-tuple-element.464, f32[1,512,12,64]{1,0,3,2:T(1,128)} %copy.209, s32[]{:T(128)S(6)} %copy.228, s32[]{:T(128)} %constant.41.clone.1..sunk, s32[]{:T(128)} %constant.41.clone.1..sunk, s32[]{:T(128)} %constant.41.clone.1..sunk) | dynamic-update-slice | bytes 3145732 | tf_op jit(solution)/shard_map/while/body/jit(dynamic_update_index_in_dim)/dynamic_update_slice | solution.py:144
  275.1 28.8 %dynamic_update_slice.28 = f32[2,512,12,64]{1,0,3,2:T(2,128)} dynamic-update-slice(f32[2,512,12,64]{1,0,3,2:T(2,128)} %get-tuple-element.463, f32[1,512,12,64]{1,0,3,2:T(1,128)} %copy.208, s32[]{:T(128)S(6)} %copy.228, s32[]{:T(128)} %constant.41.clone.1..sunk, s32[]{:T(128)} %constant.41.clone.1..sunk, s32[]{:T(128)} %constant.41.clone.1..sunk) | dynamic-update-slice | bytes 3145732 | tf_op jit(solution)/shard_map/while/body/jit(dynamic_update_index_in_dim)/dynamic_update_slice | solution.py:144
  311.5 6.9 multiply_reduce_fusion.4
  318.3 7.1 multiply_convert_fusion.3
  334.2 28.8 %dynamic_update_slice.29 = f32[2,512,12,64]{1,0,3,2:T(2,128)} dynamic-update-slice(f32[2,512,12,64]{1,0,3,2:T(2,128)} %get-tuple-element.464, f32[1,512,12,64]{1,0,3,2:T(1,128)} %copy.209, s32[]{:T(128)S(6)} %copy.228, s32[]{:T(128)} %constant.41.clone.1..sunk, s32[]{:T(128)} %constant.41.clone.1..sunk, s32[]{:T(128)} %constant.41.clone.1..sunk) | dynamic-update-slice | bytes 3145732 | tf_op jit(solution)/shard_map/while/body/jit(dynamic_update_index_in_dim)/dynamic_update_slice | solution.py:144
  363.0 28.8 %dynamic_update_slice.28 = f32[2,512,12,64]{1,0,3,2:T(2,128)} dynamic-update-slice(f32[2,512,12,64]{1,0,3,2:T(2,128)} %get-tuple-element.463, f32[1,512,12,64]{1,0,3,2:T(1,128)} %copy.208, s32[]{:T(128)S(6)} %copy.228, s32[]{:T(128)} %constant.41.clone.1..sunk, s32[]{:T(128)} %constant.41.clone.1..sunk, s32[]{:T(128)} %constant.41.clone.1..sunk) | dynamic-update-slice | bytes 3145732 | tf_op jit(solution)/shard_map/while/body/jit(dynamic_update_index_in_dim)/dynamic_update_slice | solution.py:144
  441.0 10.1 fusion.78
  451.1 30.3 %multiply_convert_fusion.1 = (bf16[1024,4,768]{2,0,1:T(8,128)(2,1)}, f32[1024,4,768]{2,0,1:T(8,128)}) fusion(f32[1024,4,768]{2,0,1:T(8,128)S(1)} %get-tuple-element.306, f32[4,768]{1,0:T(4,128)S(1)} %copy-done.51, u8[1024,768]{1,0:T(8,128)(4,1)S(1)} %get-tuple-element.219, u8[1024,768]{1,0:T(8,128)(4,1)S(1)} %get-tuple-element.218), kind=kLoop, calls=%fused_computation.68 | loop fusion | flops 223346688 | bytes 33042432 | tf_op jit(solution)/shard_map/convert_element_type | solution.py:156
  481.4 16.9 %convert_reduce_fusion = (f32[4,768]{1,0:T(4,128)S(1)}, bf16[1024,4,768]{2,0,1:T(8,128)(2,1)}) fusion(f32[1024,4,768]{2,0,1:T(8,128)} %get-tuple-element.275, bf16[1024,768,1]{1,0,2:T(8,128)(2,1)S(1)} %bitcast.318, bf16[12,768,768]{2,1,0:T(8,128)(2,1)} %all-gather.3.cloned.1.call-done, f32[1024,4,768]{2,0,1:T(8,128)} %copy-done.7, f32[4,768]{1,0:T(4,128)S(1)} %copy-done.51), kind=kOutput, calls=%fused_computation.66 | convolution fusion | flops 4885312512 | bytes 37773312 | tf_op jit(solution)/shard_map/nd,kfd->nkf/dot_general | solution.py:178
  498.3 10.0 convolution_bitcast_fusion
  508.4 7.9 fusion.131
  516.3 6.2 convolution_bitcast_fusion.1
  522.5 19.8 %pad_maximum_fusion = f32[12,768,768]{1,2,0:T(8,128)} fusion(f32[4,768,768]{1,2,0:T(8,128)} %fusion.131, f32[4,768,768]{1,2,0:T(8,128)} %convolution_bitcast_fusion, f32[1,768,768]{1,2,0:T(8,128)S(1)} %convolution_bitcast_fusion.2, f32[3,768,768]{1,2,0:T(8,128)} %convolution_bitcast_fusion.1), kind=kLoop, calls=%fused_computation.58 | loop fusion | flops 21233664 | bytes 56623104 | tf_op jit(solution)/shard_map/concatenate | solution.py:222
  542.3 33.5 %copy.146 = f32[12,768,768]{2,0,1:T(8,128)} copy(f32[12,768,768]{1,2,0:T(8,128)} %pad_maximum_fusion) | data formatting | bytes 56623104 | tf_op jit(solution)/shard_map/concatenate | solution.py:222
  578.2 10.1 fusion.54
  588.4 8.2 bitcast_reduce_fusion.1
  600.9 38.5 %all-reduce.8 = f32[13,768]{1,0:T(8,128)S(1)} all-reduce(f32[13,768]{1,0:T(8,128)S(1)} %concatenate.43), channel_id=3, replica_groups=mesh['wide'=8,'narrow'=4] {'wide','narrow'}, use_global_device_ids=true, to_apply=%region_24.25.clone | all-reduce | flops 9984 | bytes 79872
  645.0 277.6 %reduce-scatter.3.cloned.1.call-done = f32[12,24,768]{2,0,1:T(8,128)} async-done(((f32[12,768,768]{2,0,1:T(8,128)}), f32[12,24,768]{2,0,1:T(8,128)}) %reduce-scatter.3.cloned.1.call-update) | async-done | bytes 884752 | tf_op jit(solution)/shard_map/reduce_scatter | solution.py:234
  926.6 39.3 %psum.7 = f32[]{:T(128)} all-reduce(f32[]{:T(128)S(6)} %add.174), channel_id=1, replica_groups=mesh['wide'=8,'narrow'=4] {'wide','narrow'}, use_global_device_ids=true, to_apply=%region_26.27 | all-reduce | flops 1 | bytes 8 | tf_op jit(solution)/shard_map/psum | solution.py:238
  978.3 10.1 fusion.61
  988.4 17.6 %all-to-all-done = bf16[32,24,768]{2,1,0:T(8,128)(2,1)S(1)} async-done(((bf16[32,24,768]{2,1,0:T(8,128)(2,1)}), bf16[32,24,768]{2,1,0:T(8,128)(2,1)S(1)}, u32[]{:S(2)}, u32[]{:S(2)}) %all-to-all-start) | async-done | bytes 1179680 | tf_op jit(solution)/shard_map/all_to_all | solution.py:251
  1009.3 6.3 fusion.102
  1036.5 13.8 %all-to-all-done.1 = bf16[32,24,768]{2,1,0:T(8,128)(2,1)} async-done(((bf16[32,24,768]{2,1,0:T(8,128)(2,1)}), bf16[32,24,768]{2,1,0:T(8,128)(2,1)}, u32[]{:S(2)}, u32[]{:S(2)}) %all-to-all-start.1) | async-done | bytes 1179680 | tf_op jit(solution)/shard_map/all_to_all | solution.py:268
  (260 shorter events, 217.8 us)
Async XLA Ops:
  7.2 998.9 %copy-start = (f32[1,768,768]{2,1,0:T(8,128)S(1)}, f32[1,768,768]{2,1,0:T(8,128)}, u32[]{:S(2)}) copy-start(f32[1,768,768]{2,1,0:T(8,128)} %param.22) | copy-start | bytes 7077892
  7.2 110.4 %all-gather.3.cloned.1.call-start = ((), (), s32[]{:S(2)}) async-start(), calls=%async_computation.3 | async-start | bytes 14598144 | tf_op jit(solution)/shard_map/all_gather | solution.py:123
  9.4 913.2 %reduce-scatter.3.cloned.1.call-start = ((), (), s32[]{:S(2)}) async-start(), calls=%async_computation.4 | async-start | bytes 38928384 | tf_op jit(solution)/shard_map/reduce_scatter | solution.py:234
  57.7 7.4 copy-start.3
  159.9 5.2 copy-start.10
  159.9 5.2 copy-start.11
  230.5 7.1 copy-start.1
  318.3 7.1 copy-start.1
  451.1 30.3 %copy-start.7 = (f32[1024,4,768]{2,0,1:T(8,128)}, f32[1024,4,768]{2,0,1:T(8,128)S(1)}, u32[]{:S(2)}) copy-start(f32[1024,4,768]{2,0,1:T(8,128)S(1)} %get-tuple-element.306) | copy-start | bytes 37748740
  498.3 10.0 copy-start.15
  508.4 8.0 copy-start.17
  508.4 8.0 copy-start.19
  508.4 8.0 copy-start.21
  508.4 8.0 copy-start.30
  578.2 10.1 copy-start.4
  578.2 10.2 copy-start.18
  578.2 10.2 copy-start.20
  578.2 10.2 copy-start.22
  578.2 10.2 copy-start.44
  578.2 10.2 copy-start.48
  578.2 10.2 copy-start.50
  588.4 8.3 copy-start.8
  588.4 8.3 copy-start.55
  588.4 8.3 copy-start.46
  639.4 5.6 copy-start.42
  972.0 34.1 %all-to-all-start = ((bf16[32,24,768]{2,1,0:T(8,128)(2,1)}), bf16[32,24,768]{2,1,0:T(8,128)(2,1)S(1)}, u32[]{:S(2)}, u32[]{:S(2)}) async-start(bf16[32,24,768]{2,1,0:T(8,128)(2,1)} %copy.147), calls=%async_computation.1 | async-start | bytes 2359296 | tf_op jit(solution)/shard_map/all_to_all | solution.py:251
  1017.3 33.0 %all-to-all-start.1 = ((bf16[32,24,768]{2,1,0:T(8,128)(2,1)}), bf16[32,24,768]{2,1,0:T(8,128)(2,1)}, u32[]{:S(2)}, u32[]{:S(2)}) async-start(bf16[32,24,768]{2,1,0:T(8,128)(2,1)} %copy.149), calls=%async_computation.2 | async-start | bytes 2359296 | tf_op jit(solution)/shard_map/all_to_all | solution.py:268
  1021.3 5.9 copy-start.13
  1021.3 7.3 copy-start.56
  1021.3 7.3 copy-start.57
  1021.3 8.7 copy-start.27
  1033.3 17.0 %copy-start.59 = (s32[12]{0:T(128)S(1)}, s32[12]{0:T(128)}, u32[]{:S(2)}) copy-start(s32[12]{0:T(128)} %param.25) | copy-start | bytes 148
  (37 other events, 115.6 us)
Sparse Core Ops, SparseCore 0:
  11.5 106.0 all-gather.2
  576.0 346.5 reduce-scatter.2
where the time goes:
time: 1080 us; the launch traced here: 1060 us
  waiting for transfers between devices  359 us (33%)
  local copies, waits for them, and re-layouts  258 us (24%)
  matrix products  172 us (16%)
  other arithmetic  125 us (12%)
  blocking collectives  122 us (11%)
  between operations  18.2 us (2%)
    reduce_scatter x1, waiting for transfers between devices, per_device(): lax.psum_scatter(grad_blocks, ('wide', 'narrow'), scatter_dimension=1, ti...  278 us
    dynamic_update_slice x8, local copies, waits for them, and re-layouts, per_device(): lax.map(attend_forward, (queries, keys_rot, values_low, segment_ids))  126 us
    all_gather x1, waiting for transfers between devices, per_device(): lax.all_gather(blocks.astype(jnp.bfloat16), ('wide', 'narrow'), axis=1, t...  49.8 us
    all_gather x1, blocking collectives, per_device(): lax.all_gather(vectors.astype(jnp.bfloat16), ('wide', 'narrow'), axis=1,...  44 us
    psum x1, blocking collectives, per_device(): squares = lax.psum(local_squares, ('wide', 'narrow'))  39.3 us
    unnamed x1, blocking collectives  38.5 us
    concatenate x1, local copies, waits for them, and re-layouts, per_device(): jnp.concatenate([grad_qkv, grad_outproj[None], grad_up, grad_down], axis=0)  33.5 us
    convert_element_type x1, other arithmetic, per_device(): active_low = activated.astype(jnp.bfloat16)  30.3 us
  transfers between devices with their start and end apart: 4, of which 4 were waited for; matrix products, arithmetic and copies ran while one was open for 7% of the time, Pallas kernels for 0%

commit v1 on v0

v1 whole, which is shorter than its diff:
```python
import functools
import math

import jax
import jax.numpy as jnp
from jax import lax
from jax.experimental import pallas as pl
from jax.experimental.pallas import tpu as pltpu
from jax.sharding import PartitionSpec as P

H = 12
FF = 3072
ROT = 16
NPARAM = 7087872
LONGEST = 256

clip_level = 1.0
matrix_rate = 0.03
vector_rate = 0.2
decay_beta = 0.5
norm_epsilon = 1e-05

f32 = jnp.float32
bf16 = jnp.bfloat16
AXES = ("wide", "narrow")
LANES = 128
MIB = 2**20

NN = (((1,), (0,)), ((), ()))
NT = (((1,), (1,)), ((), ()))
TN = (((0,), (0,)), ((), ()))


def mm(left, right, dims):
    return lax.dot_general(left, right, dims, preferred_element_type=f32)


def call(body, flops, moved, vmem=60, **rest):
    grid = rest["grid_spec"].grid if "grid_spec" in rest else rest.get("grid", ())
    return pl.pallas_call(
        body,
        compiler_params=pltpu.CompilerParams(
            vmem_limit_bytes=vmem * MIB,
            dimension_semantics=("arbitrary",) * len(grid),
        ),
        cost_estimate=pl.CostEstimate(
            flops=int(flops), bytes_accessed=int(moved), transcendentals=0
        ),
        **rest,
    )


def sub_sum(values):
    return jnp.sum(values.reshape(-1, 8, values.shape[-1]), axis=0)


def rotary_tables(segment_ids):
    rows, length = segment_ids.shape
    start = jnp.sum(
        (segment_ids[:, None, :] < segment_ids[:, :, None]).astype(jnp.int32), axis=-1
    )
    offset = (jnp.arange(length, dtype=jnp.int32)[None] - start).astype(f32).reshape(-1, 1)
    half = ROT // 2
    lane = jnp.arange(LANES) % 64
    rates = jnp.power(10000.0, -2.0 * jnp.arange(half, dtype=f32) / ROT)
    angle = offset * jnp.where(lane < ROT, rates[lane % half], 0.0)[None]
    cosine, sine = jnp.cos(angle), jnp.sin(angle)
    first = jnp.where(lane[None] < half, -sine, 0.0)
    second = jnp.where((lane[None] >= half) & (lane[None] < ROT), sine, 0.0)
    return cosine, first, second


def rotate(values, cosine, first, second):
    parts = []
    for at in range(0, values.shape[1], LANES):
        part = values[:, at : at + LANES]
        parts.append(
            part * cosine
            + pltpu.roll(part, LANES - ROT // 2, 1) * first
            + pltpu.roll(part, ROT // 2, 1) * second
        )
    return jnp.concatenate(parts, axis=1)


def rotate_back(values, cosine, first, second):
    return (
        values * cosine
        - pltpu.roll(values, LANES - ROT // 2, 1) * first
        - pltpu.roll(values, ROT // 2, 1) * second
    )


def project_body(a1_ref, dy_ref, w_ref, vec_ref, c_ref, a_ref, b_ref, q_ref, k_ref, v_ref, do_ref):
    a1, tables = a1_ref[...], (c_ref[...], a_ref[...], b_ref[...])
    q_ref[...] = rotate(mm(a1, w_ref[0], NN) + vec_ref[4:5, :], *tables).astype(bf16)
    k_ref[...] = rotate(mm(a1, w_ref[1], NN) + vec_ref[5:6, :], *tables).astype(bf16)
    v_ref[...] = (mm(a1, w_ref[2], NN) + vec_ref[6:7, :]).astype(bf16)
    do_ref[...] = mm(dy_ref[...], w_ref[3], NT).astype(bf16)


def project(a1, dy, weights, vecs, tables, step=256):
    count, width = a1.shape
    token = pl.BlockSpec((step, width), lambda i: (i, 0))
    table = pl.BlockSpec((step, LANES), lambda i: (i, 0))
    return call(
        project_body,
        8 * count * width * width,
        12 * count * width + 8 * width * width,
        grid=(count // step,),
        in_specs=[
            token,
            token,
            pl.BlockSpec((4, width, width), lambda i: (0, 0, 0)),
            pl.BlockSpec(vecs.shape, lambda i: (0, 0)),
            table,
            table,
            table,
        ],
        out_specs=[token] * 4,
        out_shape=[jax.ShapeDtypeStruct((count, width), bf16)] * 4,
    )(a1, dy, weights, vecs, *tables)


def attend_body(
    col_ref, row_ref, q_ref, k_ref, v_ref, do_ref, c_ref, a_ref, b_ref,
    o_ref, g_ref, sum_ref, mask_ref, dk_acc, dv_acc, *, block,
):
    length = q_ref.shape[0]
    steps = length // block

    def reach(i):
        return max(0, (i * block - (LONGEST - 1)) // block * block), (i + 1) * block

    @pl.when(pl.program_id(1) == 0)
    def _():
        for i in range(steps):
            lo, hi = reach(i)
            key = lax.broadcasted_iota(jnp.int32, (hi - lo, block), 0) + lo
            query = lax.broadcasted_iota(jnp.int32, (hi - lo, block), 1) + i * block
            same = col_ref[lo:hi, :] == row_ref[0, :, i * block : hi]
            mask = jnp.where(same & (key <= query), 0.0, -jnp.inf)
            mask_ref[i, 0 : hi - lo, 0:block] = mask
            mask_ref[i, 0 : hi - lo, block:] = mask

    low = lax.broadcasted_iota(jnp.int32, (1, LANES), 1) < 64
    eighth = jnp.asarray(0.125, bf16)
    zero = jnp.zeros((), bf16)
    keys, values, grads = k_ref[...], v_ref[...], do_ref[...]
    queries = q_ref[...] * eighth
    keys_t, values_t = (keys * eighth).T, values.T

    def both(part):
        return jnp.concatenate([jnp.where(low, part, zero), jnp.where(low, zero, part)], axis=0)

    def unstack(part):
        return jnp.concatenate([part[0:64, 0:block], part[64:, block:]], axis=0).T

    dk_acc[...] = jnp.zeros_like(dk_acc)
    dv_acc[...] = jnp.zeros_like(dv_acc)
    q_sum = jnp.zeros((8, LANES), f32)
    for i in range(steps):
        lo, hi = reach(i)
        here = slice(i * block, hi)
        q2, do2 = both(queries[here]), both(grads[here])
        scores = mm(keys[lo:hi], q2, NT) + mask_ref[i, 0 : hi - lo, :]
        raised = jnp.exp(scores - jnp.max(scores, axis=0, keepdims=True))
        soft = raised * (1.0 / jnp.sum(raised, axis=0, keepdims=True))
        d_soft = mm(values[lo:hi], do2, NT)
        inner = jnp.sum(soft * d_soft, axis=0, keepdims=True)
        soft_low = soft.astype(bf16)
        d_scores = (soft * (d_soft - inner)).astype(bf16)
        o_ref[here, :] = unstack(mm(values_t[:, lo:hi], soft_low, NN)).astype(bf16)
        dq = rotate_back(
            unstack(mm(keys_t[:, lo:hi], d_scores, NN)), c_ref[here, :], a_ref[here, :], b_ref[here, :]
        ).astype(bf16)
        g_ref[0, here, :] = dq
        q_sum = q_sum + sub_sum(dq.astype(f32))
        dk_acc[lo:hi, :] += mm(d_scores, q2, NN)
        dv_acc[lo:hi, :] += mm(soft_low, do2, NN)
    dk = rotate_back(dk_acc[...], c_ref[...], a_ref[...], b_ref[...]).astype(bf16)
    dv = dv_acc[...].astype(bf16)
    g_ref[1] = dk
    g_ref[2] = dv
    sum_ref[0] = q_sum
    sum_ref[1] = sub_sum(dk.astype(f32))
    sum_ref[2] = sub_sum(dv.astype(f32))


def attend(segment_ids, q, k, v, do, tables, block=256):
    rows, length = segment_ids.shape
    count, width = q.shape
    block = min(block, length)
    token = pl.BlockSpec((length, LANES), lambda r, h: (r, h))
    table = pl.BlockSpec((length, LANES), lambda r, h: (r, 0))
    return call(
        functools.partial(attend_body, block=block),
        24 * count * length * width,
        24 * count * width,
        grid=(rows, width // LANES),
        in_specs=[
            pl.BlockSpec((length, 1), lambda r, h: (r, 0)),
            pl.BlockSpec((1, 1, length), lambda r, h: (r, 0, 0)),
            token,
            token,
            token,
            token,
            table,
            table,
            table,
        ],
        out_specs=[
            token,
            pl.BlockSpec((3, length, LANES), lambda r, h: (0, r, h)),
            pl.BlockSpec((3, 8, LANES), lambda r, h: (0, r, h)),
        ],
        out_shape=[
            jax.ShapeDtypeStruct((count, width), bf16),
            jax.ShapeDtypeStruct((3, count, width), bf16),
            jax.ShapeDtypeStruct((3, 8 * rows, width), f32),
        ],
        scratch_shapes=[
            pltpu.VMEM((length // block, length, 2 * block), f32),
            pltpu.VMEM((length, LANES), f32),
            pltpu.VMEM((length, LANES), f32),
        ],
    )(
        segment_ids.reshape(-1, 1),
        segment_ids.reshape(rows, 1, length),
        q,
        k,
        v,
        do,
        *tables,
    )


def put_grad(grad, core, outs, index, shard):
    if len(outs) == 1:
        outs[0][index] = grad
        return
    width = grad.shape[1]
    parts = grad.reshape(-1, 2, shard, width)
    even = parts[:, 0].reshape(-1, width).astype(bf16)
    odd = parts[:, 1].reshape(-1, width).astype(bf16)
    keep_ref, send_ref = outs

    @pl.when(core == 0)
    def _():
        keep_ref[index] = even
        send_ref[index] = odd

    @pl.when(core != 0)
    def _():
        keep_ref[index] = odd
        send_ref[index] = even


def grad_shapes(blocks, width, paired):
    if paired:
        return [jax.ShapeDtypeStruct((blocks, width // 2, width), bf16)] * 2
    return [jax.ShapeDtypeStruct((blocks, width, width), f32)]


def attn_grad_body(core_ref, a1_ref, o_ref, g_ref, dy_ref, *outs, shard):
    b = pl.program_id(0)

    @pl.when(b < 3)
    def _():
        put_grad(mm(a1_ref[...], g_ref[0], TN), core_ref[0], outs, 0, shard)

    @pl.when(b == 3)
    def _():
        put_grad(mm(o_ref[...], dy_ref[...], TN), core_ref[0], outs, 0, shard)


def attn_grads(core, a1, o, g, dy, shard, paired):
    count, width = a1.shape
    whole = pl.BlockSpec((count, width), lambda b, s: (0, 0))
    shapes = grad_shapes(4, width, paired)
    return call(
        functools.partial(attn_grad_body, shard=shard),
        8 * count * width * width,
        12 * count * width + 8 * width * width,
        grid_spec=pltpu.PrefetchScalarGridSpec(
            num_scalar_prefetch=1,
            grid=(4,),
            in_specs=[
                whole,
                whole,
                pl.BlockSpec((1, count, width), lambda b, s: (jnp.minimum(b, 2), 0, 0)),
                whole,
            ],
            out_specs=[pl.BlockSpec((1, *s.shape[1:]), lambda b, s: (b, 0, 0)) for s in shapes],
        ),
        out_shape=shapes,
    )(core, a1, o, g, dy)


def gelu_parts(u):
    raised = jnp.exp(-0.5 * (u * u))
    t = 1.0 / (1.0 + (0.3275911 * math.sqrt(0.5)) * jnp.abs(u))
    poly = 1.061405429 * t - 1.453152027
    poly = poly * t + 1.421413741
    poly = poly * t - 0.284496736
    poly = (poly * t + 0.254829592) * t
    tail = 0.5 * poly * raised
    return jnp.where(u < 0, tail, 1.0 - tail), raised * (1.0 / math.sqrt(2.0 * math.pi))


def mlp_body(core_ref, a2_ref, dy_ref, wu_ref, wd_ref, bu_ref, e_ref, du_ref, sum_ref, *rest, steps, shard):
    *outs, up_acc, down_acc, sum_acc = rest
    i = pl.program_id(1)
    a2, dy = a2_ref[...], dy_ref[...]
    u = mm(a2, wu_ref[0], NN) + bu_ref[0]
    de = mm(dy, wd_ref[0], NT)
    dist, density = gelu_parts(u)
    e = (u * dist).astype(bf16)
    du = (de * (dist + u * density)).astype(bf16)
    e_ref[0] = e
    du_ref[0] = du
    up, down = mm(a2, du, TN), mm(e, dy, TN)
    part = sub_sum(du.astype(f32))

    @pl.when(i == 0)
    def _():
        up_acc[...] = up
        down_acc[...] = down
        sum_acc[...] = part

    @pl.when((i > 0) & (i < steps - 1))
    def _():
        up_acc[...] += up
        down_acc[...] += down
        sum_acc[...] += part

    @pl.when(i == steps - 1)
    def _():
        put_grad(up_acc[...] + up, core_ref[0], outs, (0, 0), shard)
        put_grad(down_acc[...] + down, core_ref[0], outs, (1, 0), shard)
        sum_ref[0] = sum_acc[...] + part


def mlp(core, a2, dy, ups, downs, biases, shard, paired, step=512):
    blocks = len(ups)
    count, width = a2.shape
    steps = count // step
    wu, wd, bu = jnp.stack(ups), jnp.stack(downs), jnp.stack(biases)[:, None, :]
    token = pl.BlockSpec((step, width), lambda j, i, s: (i, 0))
    weight = pl.BlockSpec((1, width, width), lambda j, i, s: (j, 0, 0))
    hidden = pl.BlockSpec((1, step, width), lambda j, i, s: (j, i, 0))
    shapes = [
        jax.ShapeDtypeStruct((2, blocks, *s.shape[1:]), s.dtype)
        for s in grad_shapes(blocks, width, paired)
    ]
    return call(
        functools.partial(mlp_body, steps=steps, shard=shard),
        blocks * 8 * count * width * width,
        blocks * (8 * count * width + 8 * width * width),
        grid_spec=pltpu.PrefetchScalarGridSpec(
            num_scalar_prefetch=1,
            grid=(blocks, steps),
            in_specs=[
                token,
                token,
                weight,
                weight,
                pl.BlockSpec((1, 1, width), lambda j, i, s: (j, 0, 0)),
            ],
            out_specs=[hidden, hidden, pl.BlockSpec((1, 8, width), lambda j, i, s: (j, 0, 0))]
            + [pl.BlockSpec((2, 1, *s.shape[2:]), lambda j, i, s: (0, j, 0, 0)) for s in shapes],
            scratch_shapes=[
                pltpu.VMEM((width, width), f32),
                pltpu.VMEM((width, width), f32),
                pltpu.VMEM((8, width), f32),
            ],
        ),
        out_shape=[
            jax.ShapeDtypeStruct((blocks, count, width), bf16),
            jax.ShapeDtypeStruct((blocks, count, width), bf16),
            jax.ShapeDtypeStruct((blocks, 8, width), f32),
            *shapes,
        ],
    )(core, a2, dy, wu, wd, bu)


def norm_back(grad, unit, scale, gain):
    grad = grad * gain
    first = jnp.mean(grad, axis=1, keepdims=True)
    second = jnp.mean(grad * unit, axis=1, keepdims=True)
    return scale * (grad - first - unit * second)


def finish_body(*refs, splits, parts):
    x_ref, dy_ref, o_ref, g_ref, *refs = refs
    e_refs, du_refs, refs = refs[:parts], refs[parts : 2 * parts], refs[2 * parts :]
    wa_ref, wm_ref, vec_ref, out_ref, grad_ref, sum_ref = refs
    per = splits // parts
    x, dy = x_ref[...].astype(f32), dy_ref[...].astype(f32)
    acc = mm(o_ref[...], wa_ref[3], NN)
    for j in range(splits):
        acc = acc + mm(e_refs[j // per][j % per], wm_ref[splits + j], NN)
    out_ref[...] = (x + acc + (vec_ref[7:8, :] + vec_ref[8 + splits : 9 + splits, :])).astype(bf16)
    one = mm(g_ref[0], wa_ref[0], NT) + mm(g_ref[1], wa_ref[1], NT) + mm(g_ref[2], wa_ref[2], NT)
    two = mm(du_refs[0][0], wm_ref[0], NT)
    for j in range(1, splits):
        two = two + mm(du_refs[j // per][j % per], wm_ref[j], NT)
    centred = x - jnp.mean(x, axis=1, keepdims=True)
    scale = lax.rsqrt(jnp.mean(centred * centred, axis=1, keepdims=True) + norm_epsilon)
    unit = centred * scale
    grad_ref[...] = (
        dy
        + norm_back(one, unit, scale, vec_ref[0:1, :])
        + norm_back(two, unit, scale, vec_ref[2:3, :])
    ).astype(bf16)
    sums = [sub_sum(t) for t in (one * unit, one, two * unit, two, dy)]

    @pl.when(pl.program_id(0) == 0)
    def _():
        for n, s in enumerate(sums):
            sum_ref[n] = s

    @pl.when(pl.program_id(0) > 0)
    def _():
        for n, s in enumerate(sums):
            sum_ref[n] += s


def finish(x, dy, o, g, es, dus, wa, wm, vecs, step=256):
    count, width = x.shape
    parts = len(es)
    splits = sum(e.shape[0] for e in es)
    token = pl.BlockSpec((step, width), lambda i: (i, 0))

    def stacked(n):
        return pl.BlockSpec((n, step, width), lambda i: (0, i, 0))

    def resident(w):
        return pl.BlockSpec(w.shape, lambda i: (0, 0, 0), pipeline_mode=pl.Buffered(1))

    return call(
        functools.partial(finish_body, splits=splits, parts=parts),
        24 * count * width * width,
        36 * count * width + 24 * width * width,
        grid=(count // step,),
        in_specs=[token, token, token, stacked(3)]
        + [stacked(e.shape[0]) for e in es]
        + [stacked(d.shape[0]) for d in dus]
        + [resident(wa), resident(wm), pl.BlockSpec(vecs.shape, lambda i: (0, 0))],
        out_specs=[token, token, pl.BlockSpec((5, 8, width), lambda i: (0, 0, 0))],
        out_shape=[
            jax.ShapeDtypeStruct((count, width), bf16),
            jax.ShapeDtypeStruct((count, width), bf16),
            jax.ShapeDtypeStruct((5, 8, width), f32),
        ],
    )(x, dy, o, g, *es, *dus, wa, wm, vecs)


def grid_places():
    wide, narrow = lax.axis_index("wide"), lax.axis_index("narrow")
    return wide // 2, wide % 2, narrow // 2, narrow % 2


def to_place(move):
    pairs = []
    for z in range(4):
        for y in range(2):
            for x in range(2):
                for c in range(2):
                    a, b, d, e = move(z, y, x, c)
                    pairs.append((((z * 2 + y) * 2 + x) * 2 + c, ((a * 2 + b) * 2 + d) * 2 + e))
    return pairs


def over_c(value):
    return lax.ppermute(value, AXES, to_place(lambda z, y, x, c: (z, y, x, 1 - c)))


def over_x(value):
    return lax.ppermute(value, AXES, to_place(lambda z, y, x, c: (z, y, 1 - x, c)))


def over_y(value):
    return lax.ppermute(value, AXES, to_place(lambda z, y, x, c: (z, 1 - y, x, c)))


def over_z(value, by):
    return lax.ppermute(value, AXES, to_place(lambda z, y, x, c: ((z + by) % 4, y, x, c)))


def gather_order_body(place_ref, a_ref, ac_ref, b_ref, bc_ref, w_ref, v_ref, *, blocks, shard):
    t = pl.program_id(0)
    y, x, c = place_ref[1], place_ref[2], place_ref[3]
    half = a_ref.shape[-1]
    rows = blocks * shard
    for yt in range(2):
        for xt in range(2):
            ry, rx = y ^ yt, x ^ xt
            for at, own_ref, other_ref, i, j in (
                (0, a_ref, ac_ref, ry, rx),
                (half, b_ref, bc_ref, rx, ry),
            ):
                own, other = own_ref[i, j, 0], other_ref[i, j, 0]
                first = jnp.where(c == 0, own, other)
                second = jnp.where(c == 0, other, own)
                for n in range(blocks):
                    piece = jnp.concatenate(
                        [first[n * shard : (n + 1) * shard], second[n * shard : (n + 1) * shard]], axis=0
                    )
                    base = (yt * 2 + xt) * 2 * shard
                    w_ref[n, base : base + 2 * shard, at : at + half] = piece
                v_ref[0, yt, xt, 0, :, at : at + half] = first[rows:]
                v_ref[0, yt, xt, 1, :, at : at + half] = second[rows:]


def gather_staged(shards, extra):
    blocks, shard, width = shards.shape
    z, y, x, c = grid_places()
    own = jnp.concatenate([shards.reshape(blocks * shard, width), extra], axis=0)
    line = jnp.stack([own] + [over_z(own, s) for s in (1, 2, 3)])
    half = width // 2
    a, b = line[:, :, :half], line[:, :, half:]
    a, b = jnp.stack([a, over_x(a)]), jnp.stack([b, over_y(b)])
    a, b = jnp.stack([a, over_y(a)]), jnp.stack([b, over_x(b)])
    ac, bc = over_c(a), over_c(b)
    rows = own.shape[0]
    small = extra.shape[0]
    piece = pl.BlockSpec((2, 2, 1, rows, half), lambda t, s: (0, 0, lax.rem(s[0] - t + 4, 4), 0, 0))
    weights, rest = call(
        functools.partial(gather_order_body, blocks=blocks, shard=shard),
        0,
        64 * rows * width * 4,
        grid_spec=pltpu.PrefetchScalarGridSpec(
            num_scalar_prefetch=1,
            grid=(4,),
            in_specs=[piece] * 4,
            out_specs=[
                pl.BlockSpec((blocks, width // 4, width), lambda t, s: (0, t, 0)),
                pl.BlockSpec((1, 2, 2, 2, small, width), lambda t, s: (t, 0, 0, 0, 0, 0)),
            ],
        ),
        out_shape=[
            jax.ShapeDtypeStruct((blocks, width, width), bf16),
            jax.ShapeDtypeStruct((4, 2, 2, 2, small, width), bf16),
        ],
    )(jnp.stack([z, y, x, c]).astype(jnp.int32), a, ac, b, bc)
    return weights, rest.reshape(32, small, width)


def split_one_body(place_ref, keep_ref, got_ref, ka_ref, sa_ref, kb_ref, sb_ref):
    y, x = place_ref[1], place_ref[2]
    half = ka_ref.shape[-1]

    def total(yi, xi, lo):
        return keep_ref[0, :, yi, xi, :, lo : lo + half].astype(f32) + got_ref[0, :, yi, xi, :, lo : lo + half].astype(f32)

    for i in range(2):
        ka_ref[0, :, i] = total(i, x, 0)
        sa_ref[0, :, i] = total(i, 1 - x, 0).astype(bf16)
        kb_ref[0, :, i] = total(y, i, half)
        sb_ref[0, :, i] = total(1 - y, i, half).astype(bf16)


def split_two_body(place_ref, ka_ref, ga_ref, kb_ref, gb_ref, ka2_ref, sa2_ref, kb2_ref, sb2_ref):
    y, x = place_ref[1], place_ref[2]
    for mine, k_ref, g_ref, k2_ref, s2_ref in (
        (y, ka_ref, ga_ref, ka2_ref, sa2_ref),
        (x, kb_ref, gb_ref, kb2_ref, sb2_ref),
    ):
        k2_ref[0] = k_ref[0, :, mine] + g_ref[0, :, mine].astype(f32)
        s2_ref[0] = (k_ref[0, :, 1 - mine] + g_ref[0, :, 1 - mine].astype(f32)).astype(bf16)


def split_three_body(place_ref, ka_ref, ga_ref, kb_ref, gb_ref, keep_ref, *send_refs):
    z = place_ref[0]
    half = ka_ref.shape[-1]
    for s in range(4):
        at = lax.rem(z + s, 4)
        for lo, k_ref, g_ref in ((0, ka_ref, ga_ref), (half, kb_ref, gb_ref)):
            value = k_ref[0, at] + g_ref[0, at].astype(f32)
            if s == 0:
                keep_ref[0, :, lo : lo + half] = value
            else:
                send_refs[s - 1][0, :, lo : lo + half] = value.astype(bf16)


def staged(body, place, operands, shapes):
    def spec(s):
        n = len(s.shape)
        return pl.BlockSpec((1, *s.shape[1:]), lambda b, p: (b,) + (0,) * (n - 1))

    moved = sum(v.size * v.dtype.itemsize for v in operands) * 2
    return call(
        body,
        0,
        moved,
        grid_spec=pltpu.PrefetchScalarGridSpec(
            num_scalar_prefetch=1,
            grid=(operands[0].shape[0],),
            in_specs=[spec(v) for v in operands],
            out_specs=[spec(s) for s in shapes],
        ),
        out_shape=shapes,
    )(place, *operands)


def reduce_staged(keep, send, shard):
    blocks, rows, width = keep.shape
    half = width // 2
    place = jnp.stack(grid_places()).astype(jnp.int32)
    got = over_c(send)
    full = (blocks, 4, 2, 2, shard, width)

    def shape(middle, wide, kind):
        return jax.ShapeDtypeStruct((blocks, *middle, shard, wide), kind)

    ka, sa, kb, sb = staged(
        split_one_body,
        place,
        [keep.reshape(full), got.reshape(full)],
        [shape((4, 2), half, k) for k in (f32, bf16, f32, bf16)],
    )
    ga, gb = over_x(sa), over_y(sb)
    ka, sa, kb, sb = staged(
        split_two_body, place, [ka, ga, kb, gb], [shape((4,), half, k) for k in (f32, bf16, f32, bf16)]
    )
    ga, gb = over_y(sa), over_x(sb)
    own, *sends = staged(
        split_three_body, place, [ka, ga, kb, gb], [shape((), width, k) for k in (f32, bf16, bf16, bf16)]
    )
    return [own] + [over_z(v, s) for s, v in zip((1, 2, 3), sends)]


def pack_body(slot_ref, *refs, groups, per):
    terms, (shard_ref, out_ref, square_ref) = refs[: groups * per], refs[groups * per :]
    blocks = terms[0].shape[0]
    total = jnp.zeros(square_ref.shape, f32)
    for n in range(groups):
        for b in range(blocks):
            value = terms[n * per][b]
            for m in range(1, per):
                value = value + terms[n * per + m][b].astype(f32)
            shard_ref[n * blocks + b] = value
            total = total + value * value
    square_ref[...] = total

    def one(j, carry):
        b = slot_ref[j]

        @pl.when(b >= 0)
        def _():
            out_ref[j] = shard_ref[jnp.maximum(b, 0)].astype(bf16)

        @pl.when(b < 0)
        def _():
            out_ref[j] = jnp.zeros(out_ref.shape[1:], bf16)

        return carry

    lax.fori_loop(0, out_ref.shape[0], one, 0)


def pack(slots, groups):
    per = len(groups[0])
    blocks, shard, width = groups[0][0].shape
    count = slots.shape[0]
    whole = [v for g in groups for v in g]
    vmem = pl.BlockSpec(memory_space=pltpu.VMEM)
    return call(
        functools.partial(pack_body, groups=len(groups), per=per),
        0,
        sum(v.size * v.dtype.itemsize for v in whole) * 2,
        in_specs=[pl.BlockSpec(memory_space=pltpu.SMEM)] + [vmem] * len(whole),
        out_specs=[vmem] * 3,
        out_shape=[
            jax.ShapeDtypeStruct((blocks * len(groups), shard, width), f32),
            jax.ShapeDtypeStruct((count, shard, width), bf16),
            jax.ShapeDtypeStruct((shard, width), f32),
        ],
    )(slots, *whole)


def precondition_body(scale_ref, s_ref, l_ref, r_ref, p_ref, s_low, r_low):
    @pl.when(pl.program_id(0) == 0)
    def _():
        s_low[...] = (s_ref[...].astype(f32) * scale_ref[0]).astype(bf16)
        r_low[...] = r_ref[...].astype(bf16)

    left = mm(l_ref[...].astype(bf16), s_low[...], NN)
    p_ref[...] = (scale_ref[1] * mm(left.astype(bf16), r_low[...], NN)).astype(bf16)


def precondition(scales, block, left, right, step=256):
    width = block.shape[0]
    whole = pl.BlockSpec((width, width), lambda i: (0, 0))
    rows = pl.BlockSpec((step, width), lambda i: (i, 0))
    return call(
        precondition_body,
        4 * width**3,
        12 * width**2,
        grid=(width // step,),
        in_specs=[pl.BlockSpec(memory_space=pltpu.SMEM), whole, rows, whole],
        out_specs=rows,
        out_shape=jax.ShapeDtypeStruct((width, width), bf16),
        scratch_shapes=[pltpu.VMEM((width, width), bf16), pltpu.VMEM((width, width), bf16)],
    )(scales, block, left, right)


def statistics_body(has_ref, scale_ref, s_ref, l_ref, r_ref, nl_ref, nr_ref, s_low, *, step):
    i = pl.program_id(0)
    width = s_ref.shape[0]

    @pl.when(i == 0)
    def _():
        s_low[...] = (s_ref[...].astype(f32) * scale_ref[0]).astype(bf16)

    factor = (1.0 - decay_beta) * (scale_ref[1] * scale_ref[1] / width)
    at = pl.multiple_of(i * step, step)

    @pl.when(has_ref[0] != 0)
    def _():
        nl_ref[...] = decay_beta * l_ref[...] + factor * mm(s_low[pl.ds(at, step), :], s_low[...], NT)
        nr_ref[...] = decay_beta * r_ref[...] + factor * mm(s_low[:, pl.ds(at, step)], s_low[...], TN)

    @pl.when(has_ref[0] == 0)
    def _():
        nl_ref[...] = l_ref[...]
        nr_ref[...] = r_ref[...]


def statistics(has, scales, block, left, right, step=256):
    width = block.shape[0]
    whole = pl.BlockSpec((width, width), lambda i: (0, 0))
    rows = pl.BlockSpec((step, width), lambda i: (i, 0))
    smem = pl.BlockSpec(memory_space=pltpu.SMEM)
    return call(
        functools.partial(statistics_body, step=step),
        4 * width**3,
        18 * width**2,
        grid=(width // step,),
        in_specs=[smem, smem, whole, rows, rows],
        out_specs=[rows, rows],
        out_shape=[jax.ShapeDtypeStruct((width, width), f32)] * 2,
        scratch_shapes=[pltpu.VMEM((width, width), bf16)],
    )(has, scales, block, left, right)


def update_body(owner_ref, factor_ref, p_ref, shard_ref, block_ref, clip_ref, new_ref, copy_ref):
    for b in range(shard_ref.shape[0]):
        clip_ref[b] = shard_ref[b] * factor_ref[0]
        value = block_ref[b] - matrix_rate * p_ref[owner_ref[b]].astype(f32)
        new_ref[b] = value
        copy_ref[b] = value.astype(bf16)


def update(owners, factor, returned, shards, blocks):
    smem, vmem = pl.BlockSpec(memory_space=pltpu.SMEM), pl.BlockSpec(memory_space=pltpu.VMEM)
    return call(
        update_body,
        0,
        returned.size * 2 + shards.size * 18,
        in_specs=[smem, smem, vmem, vmem, vmem],
        out_specs=[vmem] * 3,
        out_shape=[
            jax.ShapeDtypeStruct(shards.shape, f32),
            jax.ShapeDtypeStruct(shards.shape, f32),
            jax.ShapeDtypeStruct(shards.shape, bf16),
        ],
    )(owners, factor, returned, shards, blocks)


def layer_inputs(tokens, vecs):
    values = tokens.astype(f32)
    centred = values - jnp.mean(values, axis=-1, keepdims=True)
    spread = jnp.mean(centred * centred, axis=-1, keepdims=True)
    unit = centred * lax.rsqrt(spread + norm_epsilon)
    one = (unit * vecs[0] + vecs[1]).astype(bf16)
    two = (unit * vecs[2] + vecs[3]).astype(bf16)
    return one, two


def to_all(value):
    return lax.all_to_all(value, AXES, split_axis=0, concat_axis=0, tiled=True)


def per_device(
    tokens,
    segment_ids,
    cotangent,
    blocks,
    vectors,
    stat_left,
    stat_right,
    root_left,
    root_right,
    vec_stat,
    owners,
    *,
    paired,
):
    rows_here, seq_len, width = tokens.shape
    count = rows_here * seq_len
    splits = FF // width
    slot_count = lax.axis_size(AXES)
    my_index = lax.axis_index(AXES)
    shard = width // slot_count
    vec_rows = vectors.shape[0]

    low_blocks, low_vectors = blocks.astype(bf16), vectors.astype(bf16)
    mlp_weights = lax.all_gather(low_blocks[4:], AXES, axis=1, tiled=True)
    if paired:
        flat = low_vectors.reshape(-1)
        extra = jnp.zeros((8, width), bf16).at[0, : flat.shape[0]].set(flat)
        attn_weights, rest = gather_staged(low_blocks[:4], extra)
        rest = rest[:, 0, : flat.shape[0]].reshape(slot_count, vec_rows, shard)
        vecs = rest.transpose(1, 0, 2).reshape(vec_rows, width).astype(f32)
    else:
        attn_weights = lax.all_gather(low_blocks[:4], AXES, axis=1, tiled=True)
        vecs = lax.all_gather(low_vectors, AXES, axis=1, tiled=True).astype(f32)

    flat_tokens = tokens.reshape(count, width)
    dy = cotangent.reshape(count, width)
    tables = rotary_tables(segment_ids)
    a1, a2 = layer_inputs(flat_tokens, vecs)
    core = (my_index % 2).astype(jnp.int32).reshape(1)

    q, k, v, do = project(a1, dy, attn_weights, vecs, tables)
    o, g, attn_sums = attend(segment_ids, q, k, v, do, tables)
    groups = [attn_grads(core, a1, o, g, dy, shard, paired)]
    es, dus, up_sums = [], [], []
    half = splits // 2
    for first in range(0, splits, half):
        which = range(first, first + half)
        e, du, up_sum, *grads = mlp(
            core,
            a2,
            dy,
            [mlp_weights[j] for j in which],
            [mlp_weights[splits + j] for j in which],
            [vecs[8 + j] for j in which],
            shard,
            paired,
        )
        es.append(e)
        dus.append(du)
        up_sums.append(up_sum)
        groups.append([v.reshape(-1, *v.shape[2:]) for v in grads])
    out, grad_in, sums = finish(flat_tokens, dy, o, g, es, dus, attn_weights, mlp_weights, vecs)

    if paired:
        terms = [reduce_staged(*group, shard) for group in groups]
    else:
        terms = [
            [lax.psum_scatter(group[0], AXES, scatter_dimension=1, tiled=True)] for group in groups
        ]
    order = [0, 1, 2, 3]
    for first in range(0, splits, half):
        order += [4 + first + j for j in range(half)] + [4 + splits + first + j for j in range(half)]

    sums = jnp.sum(sums, axis=1)
    qkv_sums = jnp.sum(attn_sums, axis=1)
    up_sums = jnp.sum(jnp.concatenate(up_sums, axis=0), axis=1)
    grad_vectors = jnp.concatenate([sums[:4], qkv_sums, sums[4:5], up_sums, sums[4:5]], axis=0)
    by_slot = grad_vectors.reshape(vec_rows, slot_count, shard).transpose(1, 0, 2)
    shard_vectors = jnp.sum(to_all(by_slot.reshape(slot_count, -1)), axis=0).reshape(vec_rows, shard)

    ordered = owners[jnp.asarray(order)]
    slot_ids = jnp.arange(slot_count, dtype=jnp.int32)
    match = ordered[None, :] == slot_ids[:, None]
    slots = jnp.sum(jnp.where(match, jnp.arange(1, len(order) + 1, dtype=jnp.int32)[None], 0), axis=1) - 1
    has_block = jnp.any(owners == my_index)
    shards, outgoing, squares = pack(slots, terms)
    local = jnp.sum(squares) + jnp.sum(shard_vectors * shard_vectors)
    everywhere = to_all(jnp.broadcast_to(local, (slot_count, LANES)))
    grad_norm = jnp.sqrt(jnp.sum(everywhere[:, 0]))
    factor = jnp.minimum(1.0, clip_level / grad_norm)
    root_count = math.sqrt(NPARAM)

    scale = factor * root_count
    power = jnp.exp2(jnp.floor(jnp.log2(jnp.maximum(scale, 1e-30)))).astype(bf16).astype(f32)
    scales = jnp.stack([power, scale / power])
    owned = to_all(outgoing).reshape(width, width)
    precond = precondition(scales, owned, root_left[0], root_right[0])
    returned = to_all(precond.reshape(slot_count, shard, width))
    new_left, new_right = statistics(
        has_block.astype(jnp.int32).reshape(1), scales, owned, stat_left[0], stat_right[0]
    )
    inverse = [order.index(b) for b in range(len(order))]
    shards = jnp.stack([shards[i] for i in inverse])
    clipped_blocks, new_blocks, blocks_copy = update(owners, factor.reshape(1), returned, shards, blocks)
    clipped_vectors = shard_vectors * factor
    scaled_vectors = clipped_vectors * root_count
    new_vec_stat = decay_beta * vec_stat + (1.0 - decay_beta) * (scaled_vectors * scaled_vectors)
    new_vectors = vectors - vector_rate * scaled_vectors * lax.rsqrt(new_vec_stat)
    return (
        out.reshape(tokens.shape),
        grad_in.reshape(tokens.shape),
        clipped_blocks,
        clipped_vectors,
        grad_norm,
        new_left[None],
        new_right[None],
        new_vec_stat,
        new_blocks,
        new_vectors,
        blocks_copy,
        new_vectors.astype(bf16),
    )


def solution(mesh):
    rows = P(AXES, None, None)
    split_rows = P(None, AXES, None)
    split_columns = P(None, AXES)
    paired = dict(mesh.shape) == {"wide": 8, "narrow": 4}
    return jax.shard_map(
        functools.partial(per_device, paired=paired),
        mesh=mesh,
        in_specs=(
            rows, P(AXES, None), rows, split_rows, split_columns,
            rows, rows, rows, rows, split_columns, P(),
        ),
        out_specs=(
            rows, rows, split_rows, split_columns, P(), rows, rows,
            split_columns, split_rows, split_columns, split_rows, split_columns,
        ),
        check_vma=False,
    )
```

time: 1080 us -> 427 us (0.40); the launches traced: 1060 us -> 425 us
  waiting for transfers between devices: 359 us -> 98 us
  local copies, waits for them, and re-layouts: 258 us -> 24.7 us
  Pallas kernels: 0 us -> 183 us
  matrix products: 172 us -> 0 us
  blocking collectives: 122 us -> 14.4 us
  other arithmetic: 125 us -> 27.1 us
  starting transfers between devices: 9.04 us -> 60 us
    reduce_scatter x1 -> x0, waiting for transfers between devices: 278 us -> none  [per_device(): lax.psum_scatter(grad_blocks, ('wide', 'narrow'), scatter_dimension=1, ti...]
    pallas_call x0 -> x20, Pallas kernels: none -> 183 us  [the longest x9 42.3 us: staged(): call(body, 0, moved, grid_spec=pltpu.PrefetchScalarGridSpec(num_scalar_pr...]
    dot_general x32 -> x0, matrix products: 172 us -> none  [the longest x1 16.9 us: per_device(): jnp.einsum('nd,kfd->nkf', grad_out, back_weights[4 + splits:4 + 2 * split...]
    dynamic_update_slice x8 -> x0, local copies, waits for them, and re-layouts: 126 us -> none  [per_device(): lax.map(attend_forward, (queries, keys_rot, values_low, segment_ids))]
    ppermute x0 -> x33, waiting for transfers between devices: none -> 52.1 us  [the longest x12 20.4 us: over_z(): lax.ppermute(value, AXES, to_place(lambda z, y, x, c: ((z + by) % 4, y, x...]
    convert_element_type x8 -> x5, other arithmetic: 56.6 us -> 4.43 us  [the longest x1 2.58 us: layer_inputs(): two = (unit * vecs[2] + vecs[3]).astype(bf16)]
    all_gather x1, waiting for transfers between devices: 49.8 us -> 0.01 us  [per_device(): mlp_weights = lax.all_gather(low_blocks[4:], AXES, axis=1, tiled=True)]
    ppermute x0 -> x33, starting transfers between devices: none -> 47.9 us  [the longest x12 30.6 us: over_z(): lax.ppermute(value, AXES, to_place(lambda z, y, x, c: ((z + by) % 4, y, x...]
  transfers between devices with their start and end apart: 4 -> 37, of which waited for: 4 -> 14; matrix products, arithmetic and copies ran while one was open for 7% -> 9% of each run, Pallas kernels for 0% -> 40%
where the time goes in v1:
time: 427 us; the launch traced here: 425 us
  Pallas kernels  183 us (43%)
  waiting for transfers between devices  98 us (23%)
  starting transfers between devices  60 us (14%)
  other arithmetic  27.1 us (6%)
  local copies, waits for them, and re-layouts  24.7 us (6%)
  between operations  18.6 us (4%)
  blocking collectives  14.4 us (3%)
    all_to_all x3, waiting for transfers between devices, to_all(): return lax.all_to_all(value, AXES, split_axis=0, concat_axis=0, tiled=True)  45.9 us
    pallas_call x9, Pallas kernels, staged(): call(body, 0, moved, grid_spec=pltpu.PrefetchScalarGridSpec(num_scalar_pr...  42.3 us
    pallas_call x2, Pallas kernels, mlp(): call(functools.partial(mlp_body, steps=steps, shard=shard), blocks * 8 *...  40.8 us
    ppermute x12, starting transfers between devices, over_z(): lax.ppermute(value, AXES, to_place(lambda z, y, x, c: ((z + by) % 4, y, x...  30.6 us
    pallas_call x1, Pallas kernels, attend(): call(functools.partial(attend_body, block=block), 24 * count * length * w...  27.2 us
    pallas_call x1, Pallas kernels, finish(): call(functools.partial(finish_body, splits=splits, parts=parts), 24 * cou...  25.4 us
    ppermute x12, waiting for transfers between devices, over_z(): lax.ppermute(value, AXES, to_place(lambda z, y, x, c: ((z + by) % 4, y, x...  20.4 us
    ppermute x8, waiting for transfers between devices, over_y(): lax.ppermute(value, AXES, to_place(lambda z, y, x, c: (z, 1 - y, x, c)))  18.2 us
  transfers between devices with their start and end apart: 37, of which 14 were waited for; matrix products, arithmetic and copies ran while one was open for 9% of the time, Pallas kernels for 40%

profile of v1, /device:TPU:0, one launch (start us, length us, event | category | flops | bytes accessed | tf_op | source)
XLA Modules:
  0.0 425.5 jit_solution(8766812559806177780)
XLA Ops:
  9.4 4.1 collective-permute-start.1
  17.3 8.0 %collective-permute-done.1 = bf16[104,768]{1,0:T(8,128)(2,1)S(1)} collective-permute-done((bf16[104,768]{1,0:T(8,128)(2,1)S(1)}, bf16[104,768]{1,0:T(8,128)(2,1)S(1)}, u32[]{:S(2)}, u32[]{:S(2)}) %collective-permute-start.1) | collective-permute-done | bytes 159776 | tf_op jit(solution)/shard_map/ppermute | solution.py:487
  40.8 13.5 %collective-permute-done.4 = bf16[2,4,104,384]{3,2,1,0:T(8,128)(2,1)S(1)} collective-permute-done((bf16[2,4,104,384]{3,2,1,0:T(8,128)(2,1)S(1)}, bf16[2,4,104,384]{3,2,1,0:T(8,128)(2,1)S(1)}, u32[]{:S(2)}, u32[]{:S(2)}) %collective-permute-start.4) | collective-permute-done | bytes 639008 | tf_op jit(solution)/shard_map/ppermute | solution.py:483
  64.0 5.2 %compare_select_fusion.9 = f32[128]{0:T(128)S(1)} fusion(f32[]{:T(128)} %bitcast.25, f32[]{:T(128)} %bitcast.26, f32[]{:T(128)} %bitcast.27, f32[]{:T(128)} %bitcast.28, f32[]{:T(128)} %bitcast.29, f32[]{:T(128)} %bitcast.31, f32[]{:T(128)} %bitcast.30, f32[]{:T(128)} %bitcast.24), kind=kLoop, calls=%fused_computation.50 | loop fusion | flops 5376 | bytes 544 | tf_op jit(solution)/shard_map/jit(_where)/select_n | solution.py:66
  72.3 6.0 %shard_map.211 = (bf16[4,768,768]{2,1,0:T(8,128)(2,1)}, bf16[4,2,2,2,8,768]{5,4,3,2,1,0:T(8,128)(2,1)}) custom-call(s32[4]{0:T(128)} %pad_add_fusion.place_ref, bf16[2,2,4,104,384]{4,3,2,1,0:T(8,128)(2,1)} %copy-done.2, bf16[2,2,4,104,384]{4,3,2,1,0:T(8,128)(2,1)} %collective-permute-done.5.ac_ref, bf16[2,2,4,104,384]{4,3,2,1,0:T(8,128)(2,1)} %pad_maximum_fusion.1.b_ref, ...), custom_call_target="tpu_custom_call" | custom-call | bytes 20447232 | tf_op jit(solution)/shard_map/pallas_call | solution.py:528
  85.1 9.9 %shard_map.212 = (bf16[1024,768]{1,0:T(8,128)(2,1)}, bf16[1024,768]{1,0:T(8,128)(2,1)}, bf16[1024,768]{1,0:T(8,128)(2,1)}, bf16[1024,768]{1,0:T(8,128)(2,1)}) custom-call(bf16[1024,768]{1,0:T(8,128)(2,1)} %get-tuple-element.168.a1_ref, bf16[1024,768]{1,0:T(8,128)(2,1)} %bitcast.120, bf16[4,768,768]{2,1,0:T(8,128)(2,1)} %get-tuple-element.93.w_ref.refs_8_, ...), custom_call_target="tpu_custom_call" | custom-call | flops 4831838208 | bytes 14155776 | tf_op jit(solution)/shard_map/pallas_call | solution.py:105
  95.0 27.2 %shard_map.213 = (bf16[1024,768]{1,0:T(8,128)(2,1)}, bf16[3,1024,768]{2,1,0:T(8,128)(2,1)}, f32[3,16,768]{2,1,0:T(8,128)}) custom-call(s32[1024,1]{1,0:T(8,128)} %bitcast.102, s32[2,1,512]{2,1,0:T(1,128)} %reshape.289.row_ref, bf16[1024,768]{1,0:T(8,128)(2,1)} %get-tuple-element.94.q_ref, bf16[1024,768]{1,0:T(8,128)(2,1)} %get-tuple-element.95.k_ref, ...), custom_call_target="tpu_custom_call" | custom-call | flops 9663676416 | bytes 18874368 | tf_op jit(solution)/shard_map/pallas_call | solution.py:195
  122.2 10.4 %shard_map.217 = (bf16[4,384,768]{2,1,0:T(8,128)(2,1)}, bf16[4,384,768]{2,1,0:T(8,128)(2,1)}) custom-call(s32[1]{0:T(128)} %bitcast.33.core_ref, bf16[1024,768]{1,0:T(8,128)(2,1)} %get-tuple-element.168.a1_ref, bf16[1024,768]{1,0:T(8,128)(2,1)} %get-tuple-element.98.refs_2_.o_ref, bf16[3,1024,768]{2,1,0:T(8,128)(2,1)} %get-tuple-element.99.refs_3_.g_ref, ...), custom_call_target="tpu_custom_call" | custom-call | flops 4831838208 | bytes 14155776 | tf_op jit(solution)/shard_map/pallas_call | solution.py:280
  133.2 6.9 %fusion.14 = (bf16[2,768,768]{2,1,0:T(8,128)(2,1)}, bf16[2,768,768]{2,1,0:T(8,128)(2,1)}, bf16[2,768,768]{2,1,0:T(8,128)(2,1)}, bf16[2,768,768]{2,1,0:T(8,128)(2,1)}) fusion(bf16[8,768,768]{2,1,0:T(8,128)(2,1)} %all-gather.2.cloned.1.call-done.refs_9_), kind=kLoop, calls=%fused_computation.67 | loop fusion | bytes 18874368 | tf_op jit(solution)/shard_map/stack | solution.py:347
  140.1 20.5 %shard_map.215 = (bf16[2,1024,768]{2,1,0:T(8,128)(2,1)}, bf16[2,1024,768]{2,1,0:T(8,128)(2,1)}, f32[2,8,768]{2,1,0:T(8,128)}, bf16[2,2,384,768]{3,2,1,0:T(8,128)(2,1)}, bf16[2,2,384,768]{3,2,1,0:T(8,128)(2,1)}) custom-call(s32[1]{0:T(128)} %bitcast.33.core_ref, bf16[1024,768]{1,0:T(8,128)(2,1)} %get-tuple-element.167.a2_ref, bf16[1024,768]{1,0:T(8,128)(2,1)} %bitcast.122, ...), custom_call_target="tpu_custom_call" | custom-call | flops 9663676416 | bytes 22020096 | tf_op jit(solution)/shard_map/pallas_call | solution.py:355
  160.6 20.3 %shard_map.214 = (bf16[2,1024,768]{2,1,0:T(8,128)(2,1)}, bf16[2,1024,768]{2,1,0:T(8,128)(2,1)}, f32[2,8,768]{2,1,0:T(8,128)}, bf16[2,2,384,768]{3,2,1,0:T(8,128)(2,1)}, bf16[2,2,384,768]{3,2,1,0:T(8,128)(2,1)}) custom-call(s32[1]{0:T(128)} %bitcast.33.core_ref, bf16[1024,768]{1,0:T(8,128)(2,1)} %get-tuple-element.167.a2_ref, bf16[1024,768]{1,0:T(8,128)(2,1)} %bitcast.123, ...), custom_call_target="tpu_custom_call" | custom-call | flops 9663676416 | bytes 22020096 | tf_op jit(solution)/shard_map/pallas_call | solution.py:355
  182.7 5.2 %shard_map.218 = (f32[4,4,2,24,384]{4,3,2,1,0:T(8,128)}, bf16[4,4,2,24,384]{4,3,2,1,0:T(8,128)(2,1)}, f32[4,4,2,24,384]{4,3,2,1,0:T(8,128)}, bf16[4,4,2,24,384]{4,3,2,1,0:T(8,128)(2,1)}) custom-call(s32[4]{0:T(128)} %pad_add_fusion.place_ref, bf16[4,4,2,2,24,768]{5,4,3,2,1,0:T(8,128)(2,1)} %bitcast.96, bf16[4,4,2,2,24,768]{5,4,3,2,1,0:T(8,128)(2,1)} %bitcast.97), custom_call_target="tpu_custom_call" | custom-call | bytes 9437184 | tf_op jit(solution)/shard_map/pallas_call | solution.py:592
  189.9 5.3 %shard_map.224 = (f32[4,4,2,24,384]{4,3,2,1,0:T(8,128)}, bf16[4,4,2,24,384]{4,3,2,1,0:T(8,128)(2,1)}, f32[4,4,2,24,384]{4,3,2,1,0:T(8,128)}, bf16[4,4,2,24,384]{4,3,2,1,0:T(8,128)(2,1)}) custom-call(s32[4]{0:T(128)} %pad_add_fusion.place_ref, bf16[4,4,2,2,24,768]{5,4,3,2,1,0:T(8,128)(2,1)} %bitcast.95, bf16[4,4,2,2,24,768]{5,4,3,2,1,0:T(8,128)(2,1)} %bitcast.43.got_ref), custom_call_target="tpu_custom_call" | custom-call | bytes 9437184 | tf_op jit(solution)/shard_map/pallas_call | solution.py:592
  197.3 5.2 %shard_map.221 = (f32[4,4,2,24,384]{4,3,2,1,0:T(8,128)}, bf16[4,4,2,24,384]{4,3,2,1,0:T(8,128)(2,1)}, f32[4,4,2,24,384]{4,3,2,1,0:T(8,128)}, bf16[4,4,2,24,384]{4,3,2,1,0:T(8,128)(2,1)}) custom-call(s32[4]{0:T(128)} %pad_add_fusion.place_ref, bf16[4,4,2,2,24,768]{5,4,3,2,1,0:T(8,128)(2,1)} %bitcast.94, bf16[4,4,2,2,24,768]{5,4,3,2,1,0:T(8,128)(2,1)} %bitcast.40.got_ref), custom_call_target="tpu_custom_call" | custom-call | bytes 9437184 | tf_op jit(solution)/shard_map/pallas_call | solution.py:592
  206.7 4.6 %shard_map.219 = (f32[4,4,24,384]{3,2,1,0:T(8,128)}, bf16[4,4,24,384]{3,2,1,0:T(8,128)(2,1)}, f32[4,4,24,384]{3,2,1,0:T(8,128)}, bf16[4,4,24,384]{3,2,1,0:T(8,128)(2,1)}) custom-call(s32[4]{0:T(128)} %pad_add_fusion.place_ref, f32[4,4,2,24,384]{4,3,2,1,0:T(8,128)} %get-tuple-element.108.ka_ref, bf16[4,4,2,24,384]{4,3,2,1,0:T(8,128)(2,1)} %copy-done.12, ...), custom_call_target="tpu_custom_call" | custom-call | bytes 7077888 | tf_op jit(solution)/shard_map/pallas_call | solution.py:592
  211.9 5.1 %collective-permute-done.26.ga_ref = bf16[4,4,2,24,384]{4,3,2,1,0:T(8,128)(2,1)S(1)} collective-permute-done((bf16[4,4,2,24,384]{4,3,2,1,0:T(8,128)(2,1)}, bf16[4,4,2,24,384]{4,3,2,1,0:T(8,128)(2,1)S(1)}, u32[]{:S(2)}, u32[]{:S(2)}) %collective-permute-start.26) | collective-permute-done | bytes 589856 | tf_op jit(solution)/shard_map/ppermute | solution.py:479
  219.3 4.6 %shard_map.225 = (f32[4,4,24,384]{3,2,1,0:T(8,128)}, bf16[4,4,24,384]{3,2,1,0:T(8,128)(2,1)}, f32[4,4,24,384]{3,2,1,0:T(8,128)}, bf16[4,4,24,384]{3,2,1,0:T(8,128)(2,1)}) custom-call(s32[4]{0:T(128)} %pad_add_fusion.place_ref, f32[4,4,2,24,384]{4,3,2,1,0:T(8,128)} %get-tuple-element.136.ka_ref, bf16[4,4,2,24,384]{4,3,2,1,0:T(8,128)(2,1)} %copy-done.9, ...), custom_call_target="tpu_custom_call" | custom-call | bytes 7077888 | tf_op jit(solution)/shard_map/pallas_call | solution.py:592
  224.5 5.1 %collective-permute-done.18.ga_ref = bf16[4,4,2,24,384]{4,3,2,1,0:T(8,128)(2,1)S(1)} collective-permute-done((bf16[4,4,2,24,384]{4,3,2,1,0:T(8,128)(2,1)}, bf16[4,4,2,24,384]{4,3,2,1,0:T(8,128)(2,1)S(1)}, u32[]{:S(2)}, u32[]{:S(2)}) %collective-permute-start.18) | collective-permute-done | bytes 589856 | tf_op jit(solution)/shard_map/ppermute | solution.py:479
  232.0 4.7 %shard_map.222 = (f32[4,4,24,384]{3,2,1,0:T(8,128)}, bf16[4,4,24,384]{3,2,1,0:T(8,128)(2,1)}, f32[4,4,24,384]{3,2,1,0:T(8,128)}, bf16[4,4,24,384]{3,2,1,0:T(8,128)(2,1)}) custom-call(s32[4]{0:T(128)} %pad_add_fusion.place_ref, f32[4,4,2,24,384]{4,3,2,1,0:T(8,128)} %get-tuple-element.122.ka_ref, bf16[4,4,2,24,384]{4,3,2,1,0:T(8,128)(2,1)} %copy-done.8, ...), custom_call_target="tpu_custom_call" | custom-call | bytes 7077888 | tf_op jit(solution)/shard_map/pallas_call | solution.py:592
  238.9 4.2 shard_map.220
  243.0 8.8 %collective-permute-start.14 = (bf16[4,24,768]{2,1,0:T(8,128)(2,1)}, bf16[4,24,768]{2,1,0:T(8,128)(2,1)S(1)}, u32[]{:S(2)}, u32[]{:S(2)}) collective-permute-start(bf16[4,24,768]{2,1,0:T(8,128)(2,1)} %get-tuple-element.117), channel_id=1, source_target_pairs={{0,8},{1,9},{2,10},{3,11},{4,12},{5,13},{6,14},{7,15},{8,16},{9,17... | collective-permute-start | bytes 442376 | tf_op jit(solution)/shard_map/ppermute | solution.py:487
  257.7 4.2 shard_map.226
  262.0 25.4 %shard_map.216 = (bf16[1024,768]{1,0:T(8,128)(2,1)}, bf16[1024,768]{1,0:T(8,128)(2,1)}, f32[5,8,768]{2,1,0:T(8,128)}) custom-call(bf16[1024,768]{1,0:T(8,128)(2,1)} %bitcast.88, bf16[1024,768]{1,0:T(8,128)(2,1)} %bitcast.124, bf16[1024,768]{1,0:T(8,128)(2,1)} %get-tuple-element.98.refs_2_.o_ref, bf16[3,1024,768]{2,1,0:T(8,128)(2,1)} %get-tuple-element.99.refs_3_.g_ref, ...), custom_call_target="tpu_custom_call" | custom-call | flops 14495514624 | bytes 42467328 | tf_op jit(solution)/shard_map/pallas_call | solution.py:440
  289.5 5.9 %all-to-all-start = ((f32[32,1,312]{2,1,0:T(1,128)}), f32[32,1,312]{2,1,0:T(1,128)S(1)}, u32[]{:S(2)}, u32[]{:S(2)}) async-start(f32[32,1,312]{2,1,0:T(1,128)} %copy.74), calls=%async_computation | async-start | bytes 98304 | tf_op jit(solution)/shard_map/all_to_all | solution.py:782
  298.1 4.2 shard_map.223
  312.9 6.7 %collective-permute-done.23.refs_6_ = bf16[4,24,768]{2,1,0:T(8,128)(2,1)S(1)} collective-permute-done((bf16[4,24,768]{2,1,0:T(8,128)(2,1)}, bf16[4,24,768]{2,1,0:T(8,128)(2,1)S(1)}, u32[]{:S(2)}, u32[]{:S(2)}) %collective-permute-start.23) | collective-permute-done | bytes 147488 | tf_op jit(solution)/shard_map/ppermute | solution.py:487
  320.3 3.9 shard_map.227
  327.0 14.4 %all_to_all.28 = f32[32,1,128]{2,1,0:T(1,128)S(1)} all-to-all(f32[32,1,128]{2,1,0:T(1,128)S(1)} %broadcast_in_dim.75), channel_id=1, replica_groups=mesh['wide'=8,'narrow'=4] {'wide','narrow'}, dimensions={0} | all-to-all | bytes 32768 | tf_op jit(solution)/shard_map/all_to_all | solution.py:782
  346.1 27.0 %all-to-all-done.2 = bf16[32,24,768]{2,1,0:T(8,128)(2,1)S(1)} async-done(((bf16[32,24,768]{2,1,0:T(8,128)(2,1)}), bf16[32,24,768]{2,1,0:T(8,128)(2,1)S(1)}, u32[]{:S(2)}, u32[]{:S(2)}) %all-to-all-start.2) | async-done | bytes 1179680 | tf_op jit(solution)/shard_map/all_to_all | solution.py:782
  374.1 6.5 %shard_map.228 = bf16[768,768]{1,0:T(8,128)(2,1)} custom-call(f32[2]{0:T(128)} %pad_maximum_fusion.6.scale_ref, bf16[768,768]{1,0:T(8,128)(2,1)} %bitcast.89, f32[768,768]{1,0:T(8,128)} %bitcast.92, f32[768,768]{1,0:T(8,128)} %bitcast.93), custom_call_target="tpu_custom_call" | custom-call | flops 1811939328 | bytes 7077888 | tf_op jit(solution)/shard_map/pallas_call | solution.py:696
  387.2 7.1 %shard_map.230 = (f32[768,768]{1,0:T(8,128)}, f32[768,768]{1,0:T(8,128)}) custom-call(s32[1]{0:T(128)} %bitcast.54.has_ref, f32[2]{0:T(128)} %pad_maximum_fusion.6.scale_ref, bf16[768,768]{1,0:T(8,128)(2,1)} %bitcast.90, f32[768,768]{1,0:T(8,128)} %bitcast.116, f32[768,768]{1,0:T(8,128)} %bitcast.117), custom_call_target="tpu_custom_call" | custom-call | flops 1811939328 | bytes 10616832 | tf_op jit(solution)/shard_map/pallas_call | solution.py:735
  394.3 18.9 %all-to-all-done.3.p_ref = bf16[32,24,768]{2,1,0:T(8,128)(2,1)S(1)} async-done(((bf16[32,24,768]{2,1,0:T(8,128)(2,1)}), bf16[32,24,768]{2,1,0:T(8,128)(2,1)S(1)}, u32[]{:S(2)}, u32[]{:S(2)}) %all-to-all-start.3) | async-done | bytes 1179680 | tf_op jit(solution)/shard_map/all_to_all | solution.py:782
  (222 shorter events, 97.9 us)
Async XLA Ops:
  7.2 126.0 %all-gather.2.cloned.1.call-start = ((), (), s32[]{:S(2)}) async-start(), calls=%async_computation.4 | async-start | bytes 9732096 | tf_op jit(solution)/shard_map/all_gather | solution.py:809
  9.4 15.9 %collective-permute-start.1 = (bf16[104,768]{1,0:T(8,128)(2,1)S(1)}, bf16[104,768]{1,0:T(8,128)(2,1)S(1)}, u32[]{:S(2)}, u32[]{:S(2)}) collective-permute-start(bf16[104,768]{1,0:T(8,128)(2,1)S(1)} %get-tuple-element.187), channel_id=1, source_target_pairs={{0,16},{1,17},{2,18},{3,19},{4,20},{5,21},{6,22},{7,23},{8,24},{9,... | collective-permute-start | bytes 479240 | tf_op jit(solution)/shard_map/ppermute | solution.py:487
  13.5 11.8 %collective-permute-start = (bf16[104,768]{1,0:T(8,128)(2,1)S(1)}, bf16[104,768]{1,0:T(8,128)(2,1)S(1)}, u32[]{:S(2)}, u32[]{:S(2)}) collective-permute-start(bf16[104,768]{1,0:T(8,128)(2,1)S(1)} %get-tuple-element.187), channel_id=1, source_target_pairs={{0,8},{1,9},{2,10},{3,11},{4,12},{5,13},{6,14},{7,15},{8,16},{9,17... | collective-permute-start | bytes 479240 | tf_op jit(solution)/shard_map/ppermute | solution.py:487
  15.1 12.5 %collective-permute-start.2 = (bf16[104,768]{1,0:T(8,128)(2,1)S(1)}, bf16[104,768]{1,0:T(8,128)(2,1)S(1)}, u32[]{:S(2)}, u32[]{:S(2)}) collective-permute-start(bf16[104,768]{1,0:T(8,128)(2,1)S(1)} %get-tuple-element.187), channel_id=1, source_target_pairs={{0,24},{1,25},{2,26},{3,27},{4,28},{5,29},{6,30},{7,31},{8,0},{9,1... | collective-permute-start | bytes 479240 | tf_op jit(solution)/shard_map/ppermute | solution.py:487
  35.8 22.9 %collective-permute-start.7 = (bf16[2,4,104,384]{3,2,1,0:T(8,128)(2,1)}, bf16[2,4,104,384]{3,2,1,0:T(8,128)(2,1)}, u32[]{:S(2)}, u32[]{:S(2)}) collective-permute-start(bf16[2,4,104,384]{3,2,1,0:T(8,128)(2,1)} %get-tuple-element.173), channel_id=1, source_target_pairs={{0,2},{1,3},{2,0},{3,1},{4,6},{5,7},{6,4},{7,5},{8,10},{9,11},{10,... | collective-permute-start | bytes 1916936 | tf_op jit(solution)/shard_map/ppermute | solution.py:479
  39.3 15.1 %collective-permute-start.4 = (bf16[2,4,104,384]{3,2,1,0:T(8,128)(2,1)S(1)}, bf16[2,4,104,384]{3,2,1,0:T(8,128)(2,1)S(1)}, u32[]{:S(2)}, u32[]{:S(2)}) collective-permute-start(bf16[2,4,104,384]{3,2,1,0:T(8,128)(2,1)S(1)} %get-tuple-element.179), channel_id=1, source_target_pairs={{0,4},{1,5},{2,6},{3,7},{4,0},{5,1},{6,2},{7,3},{8,12},{9,13},{10,... | collective-permute-start | bytes 1916936 | tf_op jit(solution)/shard_map/ppermute | solution.py:483
  56.6 15.7 %collective-permute-start.5 = (bf16[2,2,4,104,384]{4,3,2,1,0:T(8,128)(2,1)S(1)}, bf16[2,2,4,104,384]{4,3,2,1,0:T(8,128)(2,1)}, u32[]{:S(2)}, u32[]{:S(2)}) collective-permute-start(bf16[2,2,4,104,384]{4,3,2,1,0:T(8,128)(2,1)S(1)} %pad_maximum_fusion.a_ref), channel_id=1, source_target_pairs={{0,1},{1,0},{2,3},{3,2},{4,5},{5,4},{6,7},{7,6},{8,9},{9,8},{10,11... | collective-permute-start | bytes 3833864 | tf_op jit(solution)/shard_map/ppermute | solution.py:475
  132.7 48.7 %collective-permute-start.9 = (bf16[4,384,768]{2,1,0:T(8,128)(2,1)}, bf16[4,384,768]{2,1,0:T(8,128)(2,1)S(1)}, u32[]{:S(2)}, u32[]{:S(2)}) collective-permute-start(bf16[4,384,768]{2,1,0:T(8,128)(2,1)} %get-tuple-element.107), channel_id=1, source_target_pairs={{0,1},{1,0},{2,3},{3,2},{4,5},{5,4},{6,7},{7,6},{8,9},{9,8},{10,11... | collective-permute-start | bytes 7077896 | tf_op jit(solution)/shard_map/ppermute | solution.py:475
  160.6 29.4 %collective-permute-start.25 = (bf16[4,384,768]{2,1,0:T(8,128)(2,1)}, bf16[4,384,768]{2,1,0:T(8,128)(2,1)}, u32[]{:S(2)}, u32[]{:S(2)}) collective-permute-start(bf16[4,384,768]{2,1,0:T(8,128)(2,1)} %bitcast.119), channel_id=1, source_target_pairs={{0,1},{1,0},{2,3},{3,2},{4,5},{5,4},{6,7},{7,6},{8,9},{9,8},{10,11... | collective-permute-start | bytes 7077896 | tf_op jit(solution)/shard_map/ppermute | solution.py:475
  180.9 16.4 %collective-permute-start.17 = (bf16[4,384,768]{2,1,0:T(8,128)(2,1)}, bf16[4,384,768]{2,1,0:T(8,128)(2,1)}, u32[]{:S(2)}, u32[]{:S(2)}) collective-permute-start(bf16[4,384,768]{2,1,0:T(8,128)(2,1)} %bitcast.118), channel_id=1, source_target_pairs={{0,1},{1,0},{2,3},{3,2},{4,5},{5,4},{6,7},{7,6},{8,9},{9,8},{10,11... | collective-permute-start | bytes 7077896 | tf_op jit(solution)/shard_map/ppermute | solution.py:475
  188.0 16.4 %collective-permute-start.10 = (bf16[4,4,2,24,384]{4,3,2,1,0:T(8,128)(2,1)}, bf16[4,4,2,24,384]{4,3,2,1,0:T(8,128)(2,1)S(1)}, u32[]{:S(2)}, u32[]{:S(2)}) collective-permute-start(bf16[4,4,2,24,384]{4,3,2,1,0:T(8,128)(2,1)} %get-tuple-element.109), channel_id=1, source_target_pairs={{0,2},{1,3},{2,0},{3,1},{4,6},{5,7},{6,4},{7,5},{8,10},{9,11},{10,... | collective-permute-start | bytes 1769480 | tf_op jit(solution)/shard_map/ppermute | solution.py:479
  189.4 16.4 %collective-permute-start.11 = (bf16[4,4,2,24,384]{4,3,2,1,0:T(8,128)(2,1)}, bf16[4,4,2,24,384]{4,3,2,1,0:T(8,128)(2,1)S(1)}, u32[]{:S(2)}, u32[]{:S(2)}) collective-permute-start(bf16[4,4,2,24,384]{4,3,2,1,0:T(8,128)(2,1)} %get-tuple-element.111), channel_id=1, source_target_pairs={{0,4},{1,5},{2,6},{3,7},{4,0},{5,1},{6,2},{7,3},{8,12},{9,13},{10,... | collective-permute-start | bytes 1769480 | tf_op jit(solution)/shard_map/ppermute | solution.py:483
  195.2 21.8 %collective-permute-start.26 = (bf16[4,4,2,24,384]{4,3,2,1,0:T(8,128)(2,1)}, bf16[4,4,2,24,384]{4,3,2,1,0:T(8,128)(2,1)S(1)}, u32[]{:S(2)}, u32[]{:S(2)}) collective-permute-start(bf16[4,4,2,24,384]{4,3,2,1,0:T(8,128)(2,1)} %get-tuple-element.137), channel_id=1, source_target_pairs={{0,2},{1,3},{2,0},{3,1},{4,6},{5,7},{6,4},{7,5},{8,10},{9,11},{10,... | collective-permute-start | bytes 1769480 | tf_op jit(solution)/shard_map/ppermute | solution.py:479
  195.7 22.8 %collective-permute-start.27 = (bf16[4,4,2,24,384]{4,3,2,1,0:T(8,128)(2,1)}, bf16[4,4,2,24,384]{4,3,2,1,0:T(8,128)(2,1)S(1)}, u32[]{:S(2)}, u32[]{:S(2)}) collective-permute-start(bf16[4,4,2,24,384]{4,3,2,1,0:T(8,128)(2,1)} %get-tuple-element.139), channel_id=1, source_target_pairs={{0,4},{1,5},{2,6},{3,7},{4,0},{5,1},{6,2},{7,3},{8,12},{9,13},{10,... | collective-permute-start | bytes 1769480 | tf_op jit(solution)/shard_map/ppermute | solution.py:483
  202.6 27.1 %collective-permute-start.18 = (bf16[4,4,2,24,384]{4,3,2,1,0:T(8,128)(2,1)}, bf16[4,4,2,24,384]{4,3,2,1,0:T(8,128)(2,1)S(1)}, u32[]{:S(2)}, u32[]{:S(2)}) collective-permute-start(bf16[4,4,2,24,384]{4,3,2,1,0:T(8,128)(2,1)} %get-tuple-element.123), channel_id=1, source_target_pairs={{0,2},{1,3},{2,0},{3,1},{4,6},{5,7},{6,4},{7,5},{8,10},{9,11},{10,... | collective-permute-start | bytes 1769480 | tf_op jit(solution)/shard_map/ppermute | solution.py:479
  204.4 26.8 %collective-permute-start.19 = (bf16[4,4,2,24,384]{4,3,2,1,0:T(8,128)(2,1)}, bf16[4,4,2,24,384]{4,3,2,1,0:T(8,128)(2,1)S(1)}, u32[]{:S(2)}, u32[]{:S(2)}) collective-permute-start(bf16[4,4,2,24,384]{4,3,2,1,0:T(8,128)(2,1)} %get-tuple-element.125), channel_id=1, source_target_pairs={{0,4},{1,5},{2,6},{3,7},{4,0},{5,1},{6,2},{7,3},{8,12},{9,13},{10,... | collective-permute-start | bytes 1769480 | tf_op jit(solution)/shard_map/ppermute | solution.py:483
  211.3 26.7 %collective-permute-start.12 = (bf16[4,4,24,384]{3,2,1,0:T(8,128)(2,1)}, bf16[4,4,24,384]{3,2,1,0:T(8,128)(2,1)S(1)}, u32[]{:S(2)}, u32[]{:S(2)}) collective-permute-start(bf16[4,4,24,384]{3,2,1,0:T(8,128)(2,1)} %get-tuple-element.113), channel_id=1, source_target_pairs={{0,4},{1,5},{2,6},{3,7},{4,0},{5,1},{6,2},{7,3},{8,12},{9,13},{10,... | collective-permute-start | bytes 884744 | tf_op jit(solution)/shard_map/ppermute | solution.py:483
  217.0 21.0 %collective-permute-start.13 = (bf16[4,4,24,384]{3,2,1,0:T(8,128)(2,1)}, bf16[4,4,24,384]{3,2,1,0:T(8,128)(2,1)S(1)}, u32[]{:S(2)}, u32[]{:S(2)}) collective-permute-start(bf16[4,4,24,384]{3,2,1,0:T(8,128)(2,1)} %get-tuple-element.115), channel_id=1, source_target_pairs={{0,2},{1,3},{2,0},{3,1},{4,6},{5,7},{6,4},{7,5},{8,10},{9,11},{10,... | collective-permute-start | bytes 884744 | tf_op jit(solution)/shard_map/ppermute | solution.py:479
  224.0 30.1 %collective-permute-start.28 = (bf16[4,4,24,384]{3,2,1,0:T(8,128)(2,1)}, bf16[4,4,24,384]{3,2,1,0:T(8,128)(2,1)S(1)}, u32[]{:S(2)}, u32[]{:S(2)}) collective-permute-start(bf16[4,4,24,384]{3,2,1,0:T(8,128)(2,1)} %get-tuple-element.141), channel_id=1, source_target_pairs={{0,4},{1,5},{2,6},{3,7},{4,0},{5,1},{6,2},{7,3},{8,12},{9,13},{10,... | collective-permute-start | bytes 884744 | tf_op jit(solution)/shard_map/ppermute | solution.py:483
  229.7 27.3 %collective-permute-start.29 = (bf16[4,4,24,384]{3,2,1,0:T(8,128)(2,1)}, bf16[4,4,24,384]{3,2,1,0:T(8,128)(2,1)S(1)}, u32[]{:S(2)}, u32[]{:S(2)}) collective-permute-start(bf16[4,4,24,384]{3,2,1,0:T(8,128)(2,1)} %get-tuple-element.143), channel_id=1, source_target_pairs={{0,2},{1,3},{2,0},{3,1},{4,6},{5,7},{6,4},{7,5},{8,10},{9,11},{10,... | collective-permute-start | bytes 884744 | tf_op jit(solution)/shard_map/ppermute | solution.py:479
  236.7 25.2 %collective-permute-start.20 = (bf16[4,4,24,384]{3,2,1,0:T(8,128)(2,1)}, bf16[4,4,24,384]{3,2,1,0:T(8,128)(2,1)S(1)}, u32[]{:S(2)}, u32[]{:S(2)}) collective-permute-start(bf16[4,4,24,384]{3,2,1,0:T(8,128)(2,1)} %get-tuple-element.127), channel_id=1, source_target_pairs={{0,4},{1,5},{2,6},{3,7},{4,0},{5,1},{6,2},{7,3},{8,12},{9,13},{10,... | collective-permute-start | bytes 884744 | tf_op jit(solution)/shard_map/ppermute | solution.py:483
  243.0 59.2 %collective-permute-start.14 = (bf16[4,24,768]{2,1,0:T(8,128)(2,1)}, bf16[4,24,768]{2,1,0:T(8,128)(2,1)S(1)}, u32[]{:S(2)}, u32[]{:S(2)}) collective-permute-start(bf16[4,24,768]{2,1,0:T(8,128)(2,1)} %get-tuple-element.117), channel_id=1, source_target_pairs={{0,8},{1,9},{2,10},{3,11},{4,12},{5,13},{6,14},{7,15},{8,16},{9,17... | collective-permute-start | bytes 442376 | tf_op jit(solution)/shard_map/ppermute | solution.py:487
  251.9 52.1 %collective-permute-start.15 = (bf16[4,24,768]{2,1,0:T(8,128)(2,1)}, bf16[4,24,768]{2,1,0:T(8,128)(2,1)S(1)}, u32[]{:S(2)}, u32[]{:S(2)}) collective-permute-start(bf16[4,24,768]{2,1,0:T(8,128)(2,1)} %get-tuple-element.118), channel_id=1, source_target_pairs={{0,16},{1,17},{2,18},{3,19},{4,20},{5,21},{6,22},{7,23},{8,24},{9,... | collective-permute-start | bytes 442376 | tf_op jit(solution)/shard_map/ppermute | solution.py:487
  254.1 50.3 %collective-permute-start.16 = (bf16[4,24,768]{2,1,0:T(8,128)(2,1)}, bf16[4,24,768]{2,1,0:T(8,128)(2,1)S(1)}, u32[]{:S(2)}, u32[]{:S(2)}) collective-permute-start(bf16[4,24,768]{2,1,0:T(8,128)(2,1)} %get-tuple-element.119), channel_id=1, source_target_pairs={{0,24},{1,25},{2,26},{3,27},{4,28},{5,29},{6,30},{7,31},{8,0},{9,1... | collective-permute-start | bytes 442376 | tf_op jit(solution)/shard_map/ppermute | solution.py:487
  256.9 38.4 %collective-permute-start.21 = (bf16[4,4,24,384]{3,2,1,0:T(8,128)(2,1)S(1)}, bf16[4,4,24,384]{3,2,1,0:T(8,128)(2,1)S(1)}, u32[]{:S(2)}, u32[]{:S(2)}) collective-permute-start(bf16[4,4,24,384]{3,2,1,0:T(8,128)(2,1)S(1)} %copy-done.37), channel_id=1, source_target_pairs={{0,2},{1,3},{2,0},{3,1},{4,6},{5,7},{6,4},{7,5},{8,10},{9,11},{10,... | collective-permute-start | bytes 884744 | tf_op jit(solution)/shard_map/ppermute | solution.py:479
  261.9 43.6 %collective-permute-start.30 = (bf16[4,24,768]{2,1,0:T(8,128)(2,1)}, bf16[4,24,768]{2,1,0:T(8,128)(2,1)S(1)}, u32[]{:S(2)}, u32[]{:S(2)}) collective-permute-start(bf16[4,24,768]{2,1,0:T(8,128)(2,1)} %get-tuple-element.145), channel_id=1, source_target_pairs={{0,8},{1,9},{2,10},{3,11},{4,12},{5,13},{6,14},{7,15},{8,16},{9,17... | collective-permute-start | bytes 442376 | tf_op jit(solution)/shard_map/ppermute | solution.py:487
  289.5 19.3 %all-to-all-start = ((f32[32,1,312]{2,1,0:T(1,128)}), f32[32,1,312]{2,1,0:T(1,128)S(1)}, u32[]{:S(2)}, u32[]{:S(2)}) async-start(f32[32,1,312]{2,1,0:T(1,128)} %copy.74), calls=%async_computation | async-start | bytes 98304 | tf_op jit(solution)/shard_map/all_to_all | solution.py:782
  295.4 14.1 %collective-permute-start.31 = (bf16[4,24,768]{2,1,0:T(8,128)(2,1)S(1)}, bf16[4,24,768]{2,1,0:T(8,128)(2,1)S(1)}, u32[]{:S(2)}, u32[]{:S(2)}) collective-permute-start(bf16[4,24,768]{2,1,0:T(8,128)(2,1)S(1)} %copy-done.39), channel_id=1, source_target_pairs={{0,16},{1,17},{2,18},{3,19},{4,20},{5,21},{6,22},{7,23},{8,24},{9,... | collective-permute-start | bytes 442376 | tf_op jit(solution)/shard_map/ppermute | solution.py:487
  304.4 15.2 %collective-permute-start.23 = (bf16[4,24,768]{2,1,0:T(8,128)(2,1)}, bf16[4,24,768]{2,1,0:T(8,128)(2,1)S(1)}, u32[]{:S(2)}, u32[]{:S(2)}) collective-permute-start(bf16[4,24,768]{2,1,0:T(8,128)(2,1)} %get-tuple-element.132), channel_id=1, source_target_pairs={{0,16},{1,17},{2,18},{3,19},{4,20},{5,21},{6,22},{7,23},{8,24},{9,... | collective-permute-start | bytes 442376 | tf_op jit(solution)/shard_map/ppermute | solution.py:487
  305.5 14.1 %collective-permute-start.24 = (bf16[4,24,768]{2,1,0:T(8,128)(2,1)}, bf16[4,24,768]{2,1,0:T(8,128)(2,1)S(1)}, u32[]{:S(2)}, u32[]{:S(2)}) collective-permute-start(bf16[4,24,768]{2,1,0:T(8,128)(2,1)} %get-tuple-element.133), channel_id=1, source_target_pairs={{0,24},{1,25},{2,26},{3,27},{4,28},{5,29},{6,30},{7,31},{8,0},{9,1... | collective-permute-start | bytes 442376 | tf_op jit(solution)/shard_map/ppermute | solution.py:487
  341.4 31.7 %all-to-all-start.2 = ((bf16[32,24,768]{2,1,0:T(8,128)(2,1)}), bf16[32,24,768]{2,1,0:T(8,128)(2,1)S(1)}, u32[]{:S(2)}, u32[]{:S(2)}) async-start(bf16[32,24,768]{2,1,0:T(8,128)(2,1)} %get-tuple-element.153), calls=%async_computation.2 | async-start | bytes 2359296 | tf_op jit(solution)/shard_map/all_to_all | solution.py:782
  380.6 32.6 %all-to-all-start.3 = ((bf16[32,24,768]{2,1,0:T(8,128)(2,1)}), bf16[32,24,768]{2,1,0:T(8,128)(2,1)S(1)}, u32[]{:S(2)}, u32[]{:S(2)}) async-start(bf16[32,24,768]{2,1,0:T(8,128)(2,1)} %bitcast.91), calls=%async_computation.3 | async-start | bytes 2359296 | tf_op jit(solution)/shard_map/all_to_all | solution.py:782
  (45 other events, 400.8 us)
Sparse Core Ops, SparseCore 0:
  11.0 92.4 all-gather.1
